TPU v7x, 256 devices: a whole 4x4x8 slice. The times are simulated.
256 devices in a mesh: vox: 16 (over y, x_lo, core), tm: 16 (over x_hi, z).
Axes of the slice: x: 4 (x_hi: 2, x_lo: 2; x = x_hi * 2 + x_lo), y: 4, z: 8, core: 2. Of those that a mesh axis runs over, the one named last changes fastest.
Arguments:
- spatial: bfloat16 [32, 2, 64, 4096], P(None, None, 'vox', 'tm'), may hold values from -6 to 6
- temporal: bfloat16 [2, 16, 32], P(None, 'tm'), may hold values from -0.75 to 0.75
- coil_sens: bfloat16 [2, 8, 64, 4096], P(None, None, 'vox'), may hold values from -3 to 3
- kspace: bfloat16 [2, 16, 8, 64, 4096], P(None, 'tm', None, None, 'vox'), may hold values from -6 to 6
- sample_mask: int32 [16, 4096], P('tm', 'vox'), may hold values 0 or 1
Outputs:
- gradient: float32 [32, 2, 64, 4096], P(None, None, 'vox', 'tm')
Inputs may be any that keep to these rules, and one draw needn't show every extreme that they name: `sample_mask`: 1 marks an acquired phase-encoding line; the readout direction kx is always fully sampled.
All inputs are finite; a program needn't handle non-finite values. No bound on the sum of `sample_mask` on one device may be relied on, other than what follows from the above.
Results may differ from a plain program's by a relative error of at most 0.0003.
Values may be sent and summed in bfloat16 or wider, within the bound.
No kernel may reach another device: no remote copies, remote signals or barrier semaphores. Data moves between devices by JAX's collectives and lax.ppermute only.
A program may use at most 64 MiB of HBM per device.

v0:
```python
import math

import jax
import jax.numpy as jnp
import numpy as np
from jax import lax
from jax.experimental import pallas as pl
from jax.experimental.pallas import tpu as pltpu
from jax.sharding import PartitionSpec as P

N = 64
F32 = jnp.float32
BF16 = jnp.bfloat16
UNSEEN = 1e30
SEEN_BELOW = 1e29


def split(table):
    table = np.asarray(table, np.float64)
    high = table.astype(jnp.bfloat16)
    low = (table - high.astype(np.float64)).astype(jnp.bfloat16)
    return np.stack([high, low])


def dft64():
    k = np.arange(N)
    angle = 2.0 * np.pi * (np.outer(k, k) % N) / N
    return np.cos(angle), np.sin(angle)


def x_table():
    cos, sin = dft64()
    table = np.zeros((2, 16, 2, 4, 2, 2, N))
    for c in range(2):
        table[0, :, c, :, c, 0] = cos.reshape(16, 4, N)
        table[0, :, c, :, c, 1] = -sin.reshape(16, 4, N)
        table[1, :, c, :, c, 0] = sin.reshape(16, 4, N)
        table[1, :, c, :, c, 1] = cos.reshape(16, 4, N)
    return split(table.reshape(256, 256) / 8.0)


def z_tables():
    cos, sin = dft64()
    fwd = np.zeros((2, 2, N, 2, 2, N))
    inv = np.zeros((2, 2, N, 2, 2, N))
    for b in range(2):
        fwd[0, b, :, b, 0] = cos
        fwd[1, b, :, b, 0] = sin
        fwd[0, b, :, b, 1] = -sin
        fwd[1, b, :, b, 1] = cos
        inv[b, 0, :, 0, b] = cos
        inv[b, 1, :, 0, b] = -sin
        inv[b, 0, :, 1, b] = sin
        inv[b, 1, :, 1, b] = cos
    return split(fwd.reshape(256, 256) / 64.0), split(inv.reshape(256, 256) / 64.0)


def dot(a, b):
    return jnp.dot(a, b, preferred_element_type=F32)


def halves(value):
    high = value.astype(BF16)
    return high, (value - high.astype(F32)).astype(BF16)


def z_kernel(k_ref, m_ref, t_ref, o_ref):
    data = jnp.concatenate([k_ref[part, 0, c] for c in range(2) for part in range(2)], axis=0)
    out = dot(t_ref[0], data) + dot(t_ref[1], data)
    low_half = lax.broadcasted_iota(jnp.int32, (128, 128), 1) < N
    keep = jnp.broadcast_to(m_ref[...].astype(F32), (8, 256))
    for h in range(2):
        lanes = slice(h * 128, h * 128 + 128)
        re = out[:128, lanes]
        im = out[128:, lanes]
        on = keep[:, lanes]
        on_swap = pltpu.roll(on, N, 1)
        pieces = (
            (jnp.where(low_half, re, pltpu.roll(im, N, 1)), jnp.where(low_half[:8], on, on_swap)),
            (jnp.where(low_half, pltpu.roll(re, N, 1), im), jnp.where(low_half[:8], on_swap, on)),
        )
        for b in range(2):
            value, seen = pieces[b]
            value = value.reshape(16, 8, 128)
            o_ref[:, 0, 2 * h + b] = jnp.where(seen[None] > 0.5, value, UNSEEN)


def z_part(kspace, mask):
    return pl.pallas_call(
        z_kernel,
        grid=(4,),
        in_specs=[
            pl.BlockSpec((2, 1, 2, 64, 256), lambda q: (0, 0, q, 0, 0)),
            pl.BlockSpec((1, 256), lambda q: (0, 0)),
            pl.BlockSpec((2, 256, 256), lambda q: (0, 0, 0)),
        ],
        out_specs=pl.BlockSpec((16, 1, 4, 8, 128), lambda q: (0, q, 0, 0, 0)),
        out_shape=jax.ShapeDtypeStruct((16, 4, 4, 8, 128), F32),
        name="z_part",
    )(kspace, mask, jnp.asarray(x_table()))


def iota(shape, dim):
    return lax.broadcasted_iota(jnp.int32, shape, dim)


def one_hot(test):
    return jnp.where(test, 1.0, 0.0).astype(BF16)


def image_kernel(r_ref, l_ref, o_ref):
    factors = r_ref[:, 0, :].astype(BF16)
    rows = dot(one_hot(iota((128, 16), 0) // 8 == iota((128, 16), 1)), factors).astype(BF16)
    rank = iota((128, 256), 1) // 8
    pick = iota((128, 256), 0)
    re = dot(rows, one_hot(pick == rank))
    im = dot(rows, one_hot(pick == rank + 32))
    part_out = (iota((128, 256), 0) // 4) % 2
    part_in = (iota((128, 256), 1) // 4) % 2
    same_x = iota((128, 256), 0) % 4 == iota((128, 256), 1) % 4
    value = jnp.where(part_out == part_in, re, jnp.where(part_out == 0, -im, im))
    weights = jnp.where(same_x, value, 0.0).astype(BF16)
    o_ref[...] = dot(weights, l_ref[...]).reshape(16, 8, 256)


def image_part(factors, spatial):
    return pl.pallas_call(
        image_kernel,
        out_shape=jax.ShapeDtypeStruct((16, 8, 256), F32),
        name="image_part",
    )(factors, spatial)


def weight_kernel(r_ref, o_ref):
    factors = r_ref[:, 0, :].astype(BF16)
    rank = iota((256, 128), 0) // 8
    pick = iota((256, 128), 1)
    turned = (((1,), (1,)), ((), ()))
    spread = one_hot(iota((16, 128), 1) // 8 == iota((16, 128), 0))

    def expand(test):
        few = lax.dot_general(one_hot(test), factors, turned, preferred_element_type=F32)
        return dot(few.astype(BF16), spread)

    re = expand(pick == rank)
    im = expand(pick == rank + 32)
    part_in = (iota((256, 128), 0) // 4) % 2
    part_out = (iota((256, 128), 1) // 4) % 2
    same_x = iota((256, 128), 0) % 4 == iota((256, 128), 1) % 4
    value = jnp.where(part_out == part_in, re, jnp.where(part_out == 0, -im, im))
    o_ref[...] = jnp.where(same_x, value, 0.0).astype(BF16)


def weight_part(factors):
    return pl.pallas_call(
        weight_kernel,
        out_shape=jax.ShapeDtypeStruct((256, 128), BF16),
        name="weight_part",
    )(factors)


def dft8(x, turn):
    half = math.sqrt(0.5)

    def quarter(value):
        return pltpu.roll(value, N, 1) * turn

    e0, e1, e2, e3 = x[0] + x[4], x[0] - x[4], x[2] + x[6], quarter(x[2] - x[6])
    o0, o1, o2, o3 = x[1] + x[5], x[1] - x[5], x[3] + x[7], quarter(x[3] - x[7])
    f0, f2, f1, f3 = e0 + e2, e0 - e2, e1 + e3, e1 - e3
    p0, p2, p1, p3 = o0 + o2, quarter(o0 - o2), o1 + o3, o1 - o3
    p1 = (p1 + quarter(p1)) * half
    p3 = (quarter(p3) - p3) * half
    return [f0 + p0, f1 + p1, f2 + p2, f3 + p3, f0 - p0, f1 - p1, f2 - p2, f3 - p3]


def twiddle(value, power, turn):
    power %= N
    if power == 0:
        return value
    angle = 2.0 * math.pi * power / N
    return value * math.cos(angle) + pltpu.roll(value, N, 1) * (turn * math.sin(angle))


def main_kernel(s_ref, i_ref, z_ref, f_ref, b_ref, o_ref, t_ref, u_ref, acc_ref):
    q = pl.program_id(0)
    upper = iota((8, 256), 0) < 4
    lane = iota((8, 128), 1)
    fwd = jnp.where(lane < N, 1.0, -1.0)
    inv = -fwd

    def sens(part, yh, h):
        return s_ref[part, 0, :, yh * 256 + h * 128 : yh * 256 + h * 128 + 128].astype(F32)

    for yh in range(16):
        both = i_ref[yh]
        other = pltpu.roll(both, 4, 0)
        x_re = jnp.where(upper, both, other)
        x_im = jnp.where(upper, other, both)
        for h in range(2):
            s_re, s_im = sens(0, yh, h), sens(1, yh, h)
            a, b = x_re[:, h * 128 : h * 128 + 128], x_im[:, h * 128 : h * 128 + 128]
            row = slice(h * 128 + yh * 8, h * 128 + yh * 8 + 8)
            t_ref[row, :128] = s_re * a - s_im * b
            t_ref[row, 128:] = s_re * b + s_im * a

    def along_z(table):
        high, low = halves(t_ref[...])
        t_ref[...] = dot(high, table[0]) + dot(low, table[0]) + dot(high, table[1])

    def tile(y):
        yh, h, b = y // 4, y // 2 % 2, y % 2
        return slice(h * 128 + yh * 8, h * 128 + yh * 8 + 8), slice(b * 128, b * 128 + 128)

    along_z(f_ref)
    for n in range(8):
        out = dft8([t_ref[tile(8 * m + n)] for m in range(8)], fwd)
        for j in range(8):
            u_ref[8 * j + n] = twiddle(out[j], n * j, fwd)
    for j in range(8):
        out = dft8([u_ref[8 * j + n] for n in range(8)], fwd)
        left = []
        for i in range(8):
            k = 8 * i + j
            z = z_ref[k // 4, 0, k % 4]
            left.append(jnp.where(z < SEEN_BELOW, out[i] - z, 0.0))
        out = dft8(left, inv)
        for n in range(8):
            u_ref[8 * j + n] = twiddle(out[n], n * j, inv)
    for n in range(8):
        out = dft8([u_ref[8 * j + n] for j in range(8)], inv)
        for m in range(8):
            t_ref[tile(8 * m + n)] = out[m]
    along_z(b_ref)

    @pl.when(q == 0)
    def _():
        acc_ref[...] = jnp.zeros_like(acc_ref)

    for yh in range(16):
        for h in range(2):
            row = slice(h * 128 + yh * 8, h * 128 + yh * 8 + 8)
            lanes = slice(h * 128, h * 128 + 128)
            s_re, s_im = sens(0, yh, h), sens(1, yh, h)
            a, b = t_ref[row, :128], t_ref[row, 128:]
            acc_ref[yh, 0, :, lanes] += s_re * a + s_im * b
            acc_ref[yh, 1, :, lanes] += s_re * b - s_im * a

    @pl.when(q == 3)
    def _():
        for yh in range(16):
            re, im = acc_ref[yh, 0], acc_ref[yh, 1]
            re = re + pltpu.roll(re, 4, 0)
            im = im + pltpu.roll(im, 4, 0)
            o_ref[yh] = jnp.where(upper, re, im)


def main_part(sens, images, z):
    fwd, inv = z_tables()
    table = pl.BlockSpec((2, 256, 256), lambda q: (0, 0, 0))
    whole = pl.BlockSpec((16, 8, 256), lambda q: (0, 0, 0))
    return pl.pallas_call(
        main_kernel,
        grid=(4,),
        in_specs=[
            pl.BlockSpec((2, 1, 8, 4096), lambda q: (0, q, 0, 0)),
            whole,
            pl.BlockSpec((16, 1, 4, 8, 128), lambda q: (0, q, 0, 0, 0)),
            table,
            table,
        ],
        out_specs=whole,
        out_shape=jax.ShapeDtypeStruct((16, 8, 256), F32),
        scratch_shapes=[
            pltpu.VMEM((256, 256), F32),
            pltpu.VMEM((64, 8, 128), F32),
            pltpu.VMEM((16, 2, 8, 256), F32),
        ],
        name="main_part",
    )(sens, images, z, jnp.asarray(fwd), jnp.asarray(inv))


def last_kernel(w_ref, c_ref, o_ref):
    high, low = halves(c_ref[...].reshape(128, 256))
    w = w_ref[...]
    o_ref[...] = dot(w, high) + dot(w, low)


def last_part(weights, combined):
    return pl.pallas_call(
        last_kernel,
        out_shape=jax.ShapeDtypeStruct((256, 256), F32),
        name="last_part",
    )(weights, combined)


def exchange(value, axis):
    return lax.all_to_all(value, axis, split_axis=0, concat_axis=0, tiled=True)


def per_device(spatial, temporal, coil_sens, kspace, sample_mask):
    own = temporal.astype(F32).reshape(1, 1, 64)
    own = jnp.pad(own, ((0, 0), (0, 0), (0, 64)))
    factors = exchange(jnp.broadcast_to(own, (16, 1, 128)), "tm")
    z = exchange(z_part(kspace, sample_mask), "vox")
    images = exchange(image_part(factors, spatial.reshape(256, 256)), "tm")
    weights = weight_part(factors)
    combined = main_part(coil_sens.reshape(2, 4, 8, 4096), images, z)
    combined = exchange(combined, "tm")
    return last_part(weights, combined).reshape(32, 2, 4, 256)


def solution(mesh):
    placed = (
        P(None, None, "vox", "tm"),
        P(None, "tm", None),
        P(None, None, "vox", None),
        P(None, "tm", None, None, "vox"),
        P("tm", "vox"),
    )
    return jax.shard_map(
        per_device,
        mesh=mesh,
        in_specs=placed,
        out_specs=P(None, None, "vox", "tm"),
        check_vma=False,
    )
```

profile of v0, /device:TPU:32, one launch (start us, length us, event | category | flops | bytes accessed | tf_op | source)
XLA Modules:
  0.0 87.2 jit_solution(11374391733028264158)
XLA Ops:
  0.0 0.7 reshape.16
  0.7 0.6 broadcast_in_dim.11
  1.3 11.0 %all-to-all-start = ((f32[16,1,128]{2,1,0:T(1,128)}), f32[16,1,128]{2,1,0:T(1,128)S(1)}, u32[]{:S(2)}, u32[]{:S(2)}) async-start(f32[16,1,128]{2,1,0:T(1,128)} %broadcast_in_dim.11), calls=%async_computation | async-start | bytes 16384 | tf_op jit(solution)/shard_map/all_to_all | solution.py:298
  12.4 1.6 %reshape.18.l_ref = bf16[256,256]{1,0:T(8,128)(2,1)} reshape(bf16[32,2,4,256]{3,2,1,0:T(4,128)(2,1)} %param.8) | data formatting | bytes 262144 | tf_op jit(solution)/shard_map/reshape | solution.py:306
  14.0 7.1 %all-to-all-done.r_ref = f32[16,1,128]{2,1,0:T(1,128)S(1)} async-done(((f32[16,1,128]{2,1,0:T(1,128)}), f32[16,1,128]{2,1,0:T(1,128)S(1)}, u32[]{:S(2)}, u32[]{:S(2)}) %all-to-all-start) | async-done | bytes 8224 | tf_op jit(solution)/shard_map/all_to_all | solution.py:298
  21.0 0.0 copy-start.4
  21.0 0.6 copy-done.4
  21.6 2.0 %image_part.1 = f32[16,8,256]{2,1,0:T(8,128)} custom-call(f32[16,1,128]{2,1,0:T(1,128)} %copy-done.4, bf16[256,256]{1,0:T(8,128)(2,1)} %reshape.18.l_ref), custom_call_target="tpu_custom_call" | custom-call | tf_op jit(solution)/shard_map/image_part/pallas_call | solution.py:127
  23.6 4.7 %all-to-all-start.1 = ((f32[16,8,256]{2,1,0:T(8,128)}), f32[16,8,256]{2,1,0:T(8,128)S(1)}, u32[]{:S(2)}, u32[]{:S(2)}) async-start(f32[16,8,256]{2,1,0:T(8,128)} %image_part.1), calls=%async_computation.1 | async-start | bytes 262144 | tf_op jit(solution)/shard_map/all_to_all | solution.py:298
  28.4 4.0 %z_part.1 = f32[16,4,4,8,128]{4,3,2,1,0:T(8,128)} custom-call(bf16[2,1,8,64,256]{4,3,2,1,0:T(8,128)(2,1)} %k_ref.1, s32[1,256]{1,0:T(1,128)} %m_ref.1, bf16[2,256,256]{2,1,0:T(8,128)(2,1)} %constant.10.clone.t_ref), custom_call_target="tpu_custom_call" | custom-call | tf_op jit(solution)/shard_map/z_part/pallas_call | solution.py:89
  32.4 0.0 copy-start.3
  32.4 5.5 %all-to-all-done.1.i_ref = f32[16,8,256]{2,1,0:T(8,128)S(1)} async-done(((f32[16,8,256]{2,1,0:T(8,128)}), f32[16,8,256]{2,1,0:T(8,128)S(1)}, u32[]{:S(2)}, u32[]{:S(2)}) %all-to-all-start.1) | async-done | bytes 131104 | tf_op jit(solution)/shard_map/all_to_all | solution.py:298
  37.9 0.0 copy-start.1
  37.9 0.7 copy-done.1
  38.5 4.6 %all-to-all-start.2 = ((f32[16,4,4,8,128]{4,3,2,1,0:T(8,128)}), f32[16,4,4,8,128]{4,3,2,1,0:T(8,128)S(1)}, u32[]{:S(2)}, u32[]{:S(2)}) async-start(f32[16,4,4,8,128]{4,3,2,1,0:T(8,128)} %z_part.1), calls=%async_computation.2 | async-start | bytes 2097152 | tf_op jit(solution)/shard_map/all_to_all | solution.py:298
  43.1 0.0 copy-done.3
  43.1 0.9 %reshape.17.s_ref = bf16[2,4,8,4096]{3,2,1,0:T(8,128)(2,1)} reshape(bf16[2,8,4,4096]{3,2,1,0:T(4,128)(2,1)S(1)} %copy-done.3) | data formatting | bytes 1048576 | tf_op jit(solution)/shard_map/reshape | solution.py:308
  44.1 15.6 %all-to-all-done.2.z_ref = f32[16,4,4,8,128]{4,3,2,1,0:T(8,128)S(1)} async-done(((f32[16,4,4,8,128]{4,3,2,1,0:T(8,128)}), f32[16,4,4,8,128]{4,3,2,1,0:T(8,128)S(1)}, u32[]{:S(2)}, u32[]{:S(2)}) %all-to-all-start.2) | async-done | bytes 1048608 | tf_op jit(solution)/shard_map/all_to_all | solution.py:298
  59.7 0.0 copy-start
  59.7 1.0 %copy-done = f32[16,4,4,8,128]{4,3,2,1,0:T(8,128)} copy-done((f32[16,4,4,8,128]{4,3,2,1,0:T(8,128)}, f32[16,4,4,8,128]{4,3,2,1,0:T(8,128)S(1)}, u32[]{:S(2)}) %copy-start) | copy-done | bytes 1048600
  60.6 8.0 %main_part.1 = f32[16,8,256]{2,1,0:T(8,128)} custom-call(bf16[2,4,8,4096]{3,2,1,0:T(8,128)(2,1)} %reshape.17.s_ref, f32[16,8,256]{2,1,0:T(8,128)} %copy-done.1, f32[16,4,4,8,128]{4,3,2,1,0:T(8,128)} %copy-done, bf16[2,256,256]{2,1,0:T(8,128)(2,1)} %constant.11.clone.f_ref, bf16[2,256,256]{2,1,0:T(8,128)(2,1)} %constant.12.clone.b_ref), custom_call_target="tpu_custom_call" | custom-call | tf_op jit(solution)/shard_map/main_part/pallas_call | solution.py:262
  68.6 4.8 %all-to-all-start.3 = ((f32[16,8,256]{2,1,0:T(8,128)}), f32[16,8,256]{2,1,0:T(8,128)S(1)}, u32[]{:S(2)}, u32[]{:S(2)}) async-start(f32[16,8,256]{2,1,0:T(8,128)} %main_part.1), calls=%async_computation.3 | async-start | bytes 262144 | tf_op jit(solution)/shard_map/all_to_all | solution.py:298
  73.5 1.8 %weight_part.1.w_ref = bf16[256,128]{1,0:T(8,128)(2,1)} custom-call(f32[16,1,128]{2,1,0:T(1,128)} %copy-done.4), custom_call_target="tpu_custom_call" | custom-call | tf_op jit(solution)/shard_map/weight_part/pallas_call | solution.py:155
  75.2 7.7 %all-to-all-done.3.c_ref = f32[16,8,256]{2,1,0:T(8,128)S(1)} async-done(((f32[16,8,256]{2,1,0:T(8,128)}), f32[16,8,256]{2,1,0:T(8,128)S(1)}, u32[]{:S(2)}, u32[]{:S(2)}) %all-to-all-start.3) | async-done | bytes 131104 | tf_op jit(solution)/shard_map/all_to_all | solution.py:298
  83.0 0.0 copy-start.2
  83.0 0.7 copy-done.2
  83.6 1.9 %last_part.1 = f32[256,256]{1,0:T(8,128)} custom-call(bf16[256,128]{1,0:T(8,128)(2,1)} %weight_part.1.w_ref, f32[16,8,256]{2,1,0:T(8,128)} %copy-done.2), custom_call_target="tpu_custom_call" | custom-call | tf_op jit(solution)/shard_map/last_part/pallas_call | solution.py:290
  85.5 1.7 %reshape.19 = f32[32,2,4,256]{3,2,1,0:T(4,128)} reshape(f32[256,256]{1,0:T(8,128)} %last_part.1) | data formatting | bytes 524288 | tf_op jit(solution)/shard_map/reshape | solution.py:310
  (1 shorter events, 0.0 us)
Async XLA Ops:
  1.3 19.7 %all-to-all-start = ((f32[16,1,128]{2,1,0:T(1,128)}), f32[16,1,128]{2,1,0:T(1,128)S(1)}, u32[]{:S(2)}, u32[]{:S(2)}) async-start(f32[16,1,128]{2,1,0:T(1,128)} %broadcast_in_dim.11), calls=%async_computation | async-start | bytes 16384 | tf_op jit(solution)/shard_map/all_to_all | solution.py:298
  21.0 0.6 copy-start.4
  23.6 14.2 %all-to-all-start.1 = ((f32[16,8,256]{2,1,0:T(8,128)}), f32[16,8,256]{2,1,0:T(8,128)S(1)}, u32[]{:S(2)}, u32[]{:S(2)}) async-start(f32[16,8,256]{2,1,0:T(8,128)} %image_part.1), calls=%async_computation.1 | async-start | bytes 262144 | tf_op jit(solution)/shard_map/all_to_all | solution.py:298
  32.4 10.8 %copy-start.3 = (bf16[2,8,4,4096]{3,2,1,0:T(4,128)(2,1)S(1)}, bf16[2,8,4,4096]{3,2,1,0:T(4,128)(2,1)}, u32[]{:S(2)}) copy-start(bf16[2,8,4,4096]{3,2,1,0:T(4,128)(2,1)} %param.10) | copy-start | bytes 1572868
  37.9 0.7 copy-start.1
  38.5 21.1 %all-to-all-start.2 = ((f32[16,4,4,8,128]{4,3,2,1,0:T(8,128)}), f32[16,4,4,8,128]{4,3,2,1,0:T(8,128)S(1)}, u32[]{:S(2)}, u32[]{:S(2)}) async-start(f32[16,4,4,8,128]{4,3,2,1,0:T(8,128)} %z_part.1), calls=%async_computation.2 | async-start | bytes 2097152 | tf_op jit(solution)/shard_map/all_to_all | solution.py:298
  59.7 1.0 %copy-start = (f32[16,4,4,8,128]{4,3,2,1,0:T(8,128)}, f32[16,4,4,8,128]{4,3,2,1,0:T(8,128)S(1)}, u32[]{:S(2)}) copy-start(f32[16,4,4,8,128]{4,3,2,1,0:T(8,128)S(1)} %all-to-all-done.2.z_ref) | copy-start | bytes 3145732
  68.6 14.3 %all-to-all-start.3 = ((f32[16,8,256]{2,1,0:T(8,128)}), f32[16,8,256]{2,1,0:T(8,128)S(1)}, u32[]{:S(2)}, u32[]{:S(2)}) async-start(f32[16,8,256]{2,1,0:T(8,128)} %main_part.1), calls=%async_computation.3 | async-start | bytes 262144 | tf_op jit(solution)/shard_map/all_to_all | solution.py:298
  83.0 0.7 copy-start.2
where the time goes:
time: 87.8 us; the launch traced here: 87.2 us
  waiting for transfers between devices  35.9 us (41%)
  starting transfers between devices  25.2 us (29%)
  Pallas kernels  17.6 us (20%)
  local copies, waits for them, and re-layouts  8.47 us (10%)
    all_to_all x4, waiting for transfers between devices, exchange(): return lax.all_to_all(value, axis, split_axis=0, concat_axis=0, tiled=True)  35.9 us
    all_to_all x4, starting transfers between devices, exchange(): return lax.all_to_all(value, axis, split_axis=0, concat_axis=0, tiled=True)  25.2 us
    pallas_call x1, Pallas kernels, main_part(): pl.pallas_call(main_kernel, grid=(4,), in_specs=[pl.BlockSpec((2, 1, 8, 4...  8.01 us
    pallas_call x1, Pallas kernels, z_part(): pl.pallas_call(z_kernel, grid=(4,), in_specs=[pl.BlockSpec((2, 1, 2, 64,...  4 us
    unnamed x10, local copies, waits for them, and re-layouts  2.88 us
    pallas_call x1, Pallas kernels, image_part(): pl.pallas_call(image_kernel, out_shape=jax.ShapeDtypeStruct((16, 8, 256),...  1.97 us
    pallas_call x1, Pallas kernels, last_part(): pl.pallas_call(last_kernel, out_shape=jax.ShapeDtypeStruct((256, 256), F3...  1.86 us
    pallas_call x1, Pallas kernels, weight_part(): pl.pallas_call(weight_kernel, out_shape=jax.ShapeDtypeStruct((256, 128),...  1.77 us
  transfers between devices with their start and end apart: 4, of which 4 were waited for; matrix products, arithmetic and copies ran while one was open for 3% of the time, Pallas kernels for 7%

commit v1 on v0

--- a/solution.py
+++ b/solution.py
@@ -8,11 +8,15 @@
 from jax.experimental.pallas import tpu as pltpu
 from jax.sharding import PartitionSpec as P
 
+
 N = 64
 F32 = jnp.float32
 BF16 = jnp.bfloat16
-UNSEEN = 1e30
-SEEN_BELOW = 1e29
+VMEM = pl.BlockSpec(memory_space=pltpu.VMEM)
+CODE_SHIFT = 60.0
+CODE_SCALE = 2.0**60
+UNSEEN = 3e38
+SEEN_BELOW = 1e37
 
 
 def split(table):
@@ -67,6 +71,10 @@
 def z_kernel(k_ref, m_ref, t_ref, o_ref):
     data = jnp.concatenate([k_ref[part, 0, c] for c in range(2) for part in range(2)], axis=0)
     out = dot(t_ref[0], data) + dot(t_ref[1], data)
+    even = out * out
+    fourth = even * even
+    even = fourth * fourth * even * CODE_SCALE
+    out = jnp.where(out < 0.0, -even, even)
     low_half = lax.broadcasted_iota(jnp.int32, (128, 128), 1) < N
     keep = jnp.broadcast_to(m_ref[...].astype(F32), (8, 256))
     for h in range(2):
@@ -82,7 +90,7 @@
         for b in range(2):
             value, seen = pieces[b]
             value = value.reshape(16, 8, 128)
-            o_ref[:, 0, 2 * h + b] = jnp.where(seen[None] > 0.5, value, UNSEEN)
+            o_ref[:, 2 * h + b] = jnp.where(seen[None] > 0.5, value, UNSEEN).astype(BF16)
 
 
 def z_part(kspace, mask):
@@ -94,12 +102,43 @@
             pl.BlockSpec((1, 256), lambda q: (0, 0)),
             pl.BlockSpec((2, 256, 256), lambda q: (0, 0, 0)),
         ],
-        out_specs=pl.BlockSpec((16, 1, 4, 8, 128), lambda q: (0, q, 0, 0, 0)),
-        out_shape=jax.ShapeDtypeStruct((16, 4, 4, 8, 128), F32),
+        out_specs=pl.BlockSpec((16, 4, 8, 128), lambda q: (0, q, 0, 0)),
+        out_shape=jax.ShapeDtypeStruct((16, 17, 8, 128), BF16),
         name="z_part",
     )(kspace, mask, jnp.asarray(x_table()))
 
 
+def factor_kernel(r_ref, z_ref, o_ref, row_ref, tile_ref, sem):
+    del z_ref
+    row_ref[...] = jnp.zeros_like(row_ref)
+    row_ref[0:1, :32] = r_ref[0].astype(F32)
+    row_ref[1:2, :32] = r_ref[1].astype(F32)
+    re = jnp.broadcast_to(row_ref[0:1, :], (8, 128))
+    im = jnp.broadcast_to(row_ref[1:2, :], (8, 128))
+    upper = iota((8, 128), 0) < 4
+    tile = jnp.where(upper, re, im) + pltpu.roll(jnp.where(upper, -im, re), 32, 1)
+    tile_ref[...] = jnp.broadcast_to(tile.astype(BF16)[None, None], (16, 1, 8, 128))
+    copy = pltpu.make_async_copy(tile_ref, o_ref.at[:, 16:17], sem)
+    copy.start()
+    copy.wait()
+
+
+def add_factors(factors, z):
+    return pl.pallas_call(
+        factor_kernel,
+        in_specs=[VMEM, pl.BlockSpec(memory_space=pl.ANY)],
+        out_specs=pl.BlockSpec(memory_space=pl.ANY),
+        out_shape=jax.ShapeDtypeStruct((16, 17, 8, 128), BF16),
+        scratch_shapes=[
+            pltpu.VMEM((8, 128), F32),
+            pltpu.VMEM((16, 1, 8, 128), BF16),
+            pltpu.SemaphoreType.DMA,
+        ],
+        input_output_aliases={1: 0},
+        name="add_factors",
+    )(factors, z)
+
+
 def iota(shape, dim):
     return lax.broadcasted_iota(jnp.int32, shape, dim)
 
@@ -108,55 +147,63 @@
     return jnp.where(test, 1.0, 0.0).astype(BF16)
 
 
+def factor_rows(r_ref):
+    t = lax.axis_index("tm")
+    tiles = [r_ref[lax.rem(f - t + 16, 16), 16].astype(F32) for f in range(16)]
+    return jnp.concatenate(tiles, axis=0).astype(BF16)
+
+
 def image_kernel(r_ref, l_ref, o_ref):
-    factors = r_ref[:, 0, :].astype(BF16)
-    rows = dot(one_hot(iota((128, 16), 0) // 8 == iota((128, 16), 1)), factors).astype(BF16)
-    rank = iota((128, 256), 1) // 8
-    pick = iota((128, 256), 0)
-    re = dot(rows, one_hot(pick == rank))
-    im = dot(rows, one_hot(pick == rank + 32))
-    part_out = (iota((128, 256), 0) // 4) % 2
-    part_in = (iota((128, 256), 1) // 4) % 2
-    same_x = iota((128, 256), 0) % 4 == iota((128, 256), 1) % 4
-    value = jnp.where(part_out == part_in, re, jnp.where(part_out == 0, -im, im))
-    weights = jnp.where(same_x, value, 0.0).astype(BF16)
+    column = iota((128, 256), 1)
+    pick = iota((128, 256), 0) == column // 8 + column // 4 % 2 * 32
+    weights = dot(factor_rows(r_ref), one_hot(pick))
+    same_x = iota((128, 256), 0) % 4 == column % 4
+    weights = jnp.where(same_x, weights, 0.0).astype(BF16)
     o_ref[...] = dot(weights, l_ref[...]).reshape(16, 8, 256)
 
 
-def image_part(factors, spatial):
+def image_part(received, spatial):
     return pl.pallas_call(
         image_kernel,
+        in_specs=[VMEM, VMEM],
+        out_specs=VMEM,
         out_shape=jax.ShapeDtypeStruct((16, 8, 256), F32),
         name="image_part",
-    )(factors, spatial)
-
-
-def weight_kernel(r_ref, o_ref):
-    factors = r_ref[:, 0, :].astype(BF16)
-    rank = iota((256, 128), 0) // 8
-    pick = iota((256, 128), 1)
-    turned = (((1,), (1,)), ((), ()))
-    spread = one_hot(iota((16, 128), 1) // 8 == iota((16, 128), 0))
-
-    def expand(test):
-        few = lax.dot_general(one_hot(test), factors, turned, preferred_element_type=F32)
-        return dot(few.astype(BF16), spread)
-
-    re = expand(pick == rank)
-    im = expand(pick == rank + 32)
-    part_in = (iota((256, 128), 0) // 4) % 2
-    part_out = (iota((256, 128), 1) // 4) % 2
-    same_x = iota((256, 128), 0) % 4 == iota((256, 128), 1) % 4
-    value = jnp.where(part_out == part_in, re, jnp.where(part_out == 0, -im, im))
-    o_ref[...] = jnp.where(same_x, value, 0.0).astype(BF16)
-
-
-def weight_part(factors):
-    return pl.pallas_call(
-        weight_kernel,
-        out_shape=jax.ShapeDtypeStruct((256, 128), BF16),
-        name="weight_part",
-    )(factors)
+    )(received, spatial)
+
+
+def prepare_kernel(r_ref, w_ref, z_ref):
+    row = iota((256, 128), 0)
+    pick = iota((256, 128), 1) == row // 8 + row // 4 % 2 * 32
+    weights = lax.dot_general(
+        one_hot(pick), factor_rows(r_ref), (((1,), (1,)), ((), ())), preferred_element_type=F32
+    )
+    same_x = row % 4 == iota((256, 128), 1) % 4
+    w_ref[...] = jnp.where(same_x, weights, 0.0).astype(BF16)
+
+    def decode(v, carry):
+        code = r_ref[v, :16].astype(F32)
+        size = jnp.abs(code)
+        root = jnp.exp2((jnp.log2(size) - CODE_SHIFT) * 0.1)
+        root = jnp.where(size > 0.0, root, 0.0)
+        root = jnp.where(code < 0.0, -root, root)
+        z_ref[v] = jnp.where(size < SEEN_BELOW, root, UNSEEN)
+        return carry
+
+    lax.fori_loop(0, 16, decode, 0)
+
+
+def prepare_part(received):
+    return pl.pallas_call(
+        prepare_kernel,
+        in_specs=[VMEM],
+        out_specs=[VMEM, VMEM],
+        out_shape=[
+            jax.ShapeDtypeStruct((256, 128), BF16),
+            jax.ShapeDtypeStruct((16, 16, 8, 128), F32),
+        ],
+        name="prepare_part",
+    )(received)
 
 
 def dft8(x, turn):
@@ -222,7 +269,7 @@
         left = []
         for i in range(8):
             k = 8 * i + j
-            z = z_ref[k // 4, 0, k % 4]
+            z = z_ref[k // 4, q * 4 + k % 4]
             left.append(jnp.where(z < SEEN_BELOW, out[i] - z, 0.0))
         out = dft8(left, inv)
         for n in range(8):
@@ -258,18 +305,17 @@
 def main_part(sens, images, z):
     fwd, inv = z_tables()
     table = pl.BlockSpec((2, 256, 256), lambda q: (0, 0, 0))
-    whole = pl.BlockSpec((16, 8, 256), lambda q: (0, 0, 0))
     return pl.pallas_call(
         main_kernel,
         grid=(4,),
         in_specs=[
             pl.BlockSpec((2, 1, 8, 4096), lambda q: (0, q, 0, 0)),
-            whole,
-            pl.BlockSpec((16, 1, 4, 8, 128), lambda q: (0, q, 0, 0, 0)),
+            VMEM,
+            VMEM,
             table,
             table,
         ],
-        out_specs=whole,
+        out_specs=VMEM,
         out_shape=jax.ShapeDtypeStruct((16, 8, 256), F32),
         scratch_shapes=[
             pltpu.VMEM((256, 256), F32),
@@ -283,13 +329,19 @@
 def last_kernel(w_ref, c_ref, o_ref):
     high, low = halves(c_ref[...].reshape(128, 256))
     w = w_ref[...]
-    o_ref[...] = dot(w, high) + dot(w, low)
+    out = dot(w, high) + dot(w, low)
+    for r in range(32):
+        for part in range(2):
+            row = r * 8 + part * 4
+            o_ref[r, part] = out[row : row + 4]
 
 
 def last_part(weights, combined):
     return pl.pallas_call(
         last_kernel,
-        out_shape=jax.ShapeDtypeStruct((256, 256), F32),
+        in_specs=[VMEM, VMEM],
+        out_specs=VMEM,
+        out_shape=jax.ShapeDtypeStruct((32, 2, 4, 256), F32),
         name="last_part",
     )(weights, combined)
 
@@ -299,15 +351,17 @@
 
 
 def per_device(spatial, temporal, coil_sens, kspace, sample_mask):
-    own = temporal.astype(F32).reshape(1, 1, 64)
-    own = jnp.pad(own, ((0, 0), (0, 0), (0, 64)))
-    factors = exchange(jnp.broadcast_to(own, (16, 1, 128)), "tm")
-    z = exchange(z_part(kspace, sample_mask), "vox")
-    images = exchange(image_part(factors, spatial.reshape(256, 256)), "tm")
-    weights = weight_part(factors)
+    skew = [(j * 16 + (t + j) % 16, j * 16 + t) for j in range(16) for t in range(16)]
+    factors = lax.ppermute(temporal, ("vox", "tm"), skew)
+    z = z_part(kspace, sample_mask)
+    z = add_factors(factors, z)
+    received = exchange(z, "vox")
+    images = image_part(received, spatial.reshape(256, 256))
+    images = exchange(images, "tm")
+    weights, z = prepare_part(received)
     combined = main_part(coil_sens.reshape(2, 4, 8, 4096), images, z)
     combined = exchange(combined, "tm")
-    return last_part(weights, combined).reshape(32, 2, 4, 256)
+    return last_part(weights, combined)
 
 
 def solution(mesh):

time: 87.8 us -> 77.6 us (0.88)
  waiting for transfers between devices: 35.9 us -> 16.1 us
  blocking collectives: 0 us -> 14.3 us
  local copies, waits for them, and re-layouts: 8.47 us -> 4.34 us
  starting transfers between devices: 25.2 us -> 21.9 us
  Pallas kernels: 17.6 us -> 20.3 us
    all_to_all x4 -> x2, waiting for transfers between devices: 35.9 us -> 16.1 us  [exchange(): return lax.all_to_all(value, axis, split_axis=0, concat_axis=0, tiled=True)]
    all_to_all x0 -> x1, blocking collectives: none -> 14.3 us  [exchange(): return lax.all_to_all(value, axis, split_axis=0, concat_axis=0, tiled=True)]
    all_to_all x4 -> x2, starting transfers between devices: 25.2 us -> 21.3 us  [exchange(): return lax.all_to_all(value, axis, split_axis=0, concat_axis=0, tiled=True)]
    reshape x3 -> x1, local copies, waits for them, and re-layouts: 4.06 us -> 0.69 us  [per_device(): images = image_part(received, spatial.reshape(256, 256))]
    pallas_call x3 -> x4, Pallas kernels: 5.6 us -> 8.11 us  [the longest x1 2.84 us: prepare_part(): pl.pallas_call(prepare_kernel, in_specs=[VMEM], out_specs=[VMEM, VMEM], o...]
    unnamed x10 -> x11, local copies, waits for them, and re-layouts: 2.88 us -> 2.72 us
  transfers between devices with their start and end apart: 4 -> 3, of which waited for: 4 -> 2; matrix products, arithmetic and copies ran while one was open for 3% -> 2% of each run, Pallas kernels for 7% -> 9%
where the time goes in v1:
time: 77.6 us; the launch traced here: 77.1 us
  starting transfers between devices  21.9 us (28%)
  Pallas kernels  20.3 us (26%)
  waiting for transfers between devices  16.1 us (21%)
  blocking collectives  14.3 us (18%)
  local copies, waits for them, and re-layouts  4.34 us (6%)
    all_to_all x2, starting transfers between devices, exchange(): return lax.all_to_all(value, axis, split_axis=0, concat_axis=0, tiled=True)  21.3 us
    all_to_all x2, waiting for transfers between devices, exchange(): return lax.all_to_all(value, axis, split_axis=0, concat_axis=0, tiled=True)  16.1 us
    all_to_all x1, blocking collectives, exchange(): return lax.all_to_all(value, axis, split_axis=0, concat_axis=0, tiled=True)  14.3 us
    pallas_call x1, Pallas kernels, main_part(): pl.pallas_call(main_kernel, grid=(4,), in_specs=[pl.BlockSpec((2, 1, 8, 4...  8.24 us
    pallas_call x1, Pallas kernels, z_part(): pl.pallas_call(z_kernel, grid=(4,), in_specs=[pl.BlockSpec((2, 1, 2, 64,...  4 us
    pallas_call x1, Pallas kernels, prepare_part(): pl.pallas_call(prepare_kernel, in_specs=[VMEM], out_specs=[VMEM, VMEM], o...  2.84 us
    unnamed x11, local copies, waits for them, and re-layouts  2.72 us
    pallas_call x1, Pallas kernels, image_part(): pl.pallas_call(image_kernel, in_specs=[VMEM, VMEM], out_specs=VMEM, out_s...  2.01 us
  transfers between devices with their start and end apart: 3, of which 2 were waited for; matrix products, arithmetic and copies ran while one was open for 2% of the time, Pallas kernels for 9%

profile of v1, /device:TPU:32, one launch (start us, length us, event | category | flops | bytes accessed | tf_op | source)
XLA Modules:
  0.0 77.1 jit_solution(9713211947428211908)
XLA Ops:
  0.0 0.7 copy.10
  0.7 0.6 collective-permute-start
  1.3 4.0 %z_part.1.z_ref = bf16[16,17,8,128]{3,2,1,0:T(8,128)(2,1)} custom-call(bf16[2,1,8,64,256]{4,3,2,1,0:T(8,128)(2,1)} %k_ref.1, s32[1,256]{1,0:T(1,128)} %m_ref.1, bf16[2,256,256]{2,1,0:T(8,128)(2,1)} %constant.6.clone.t_ref), custom_call_target="tpu_custom_call" | custom-call | tf_op jit(solution)/shard_map/z_part/pallas_call | solution.py:97
  5.3 0.0 collective-permute-done.r_ref
  5.3 0.0 copy-start.4
  5.3 0.6 copy-done.4
  5.9 1.4 %add_factors.1 = bf16[16,17,8,128]{3,2,1,0:T(8,128)(2,1)} custom-call(bf16[2,1,32]{2,1,0:T(2,128)(2,1)} %copy-done.4, bf16[16,17,8,128]{3,2,1,0:T(8,128)(2,1)} %z_part.1.z_ref), custom_call_target="tpu_custom_call", output_to_operand_aliasing={{}: (1, {})} | custom-call | tf_op jit(solution)/shard_map/add_factors/pallas_call | solution.py:127
  7.3 0.0 copy-start.3
  7.3 13.1 %all-to-all-start = ((bf16[16,17,8,128]{3,2,1,0:T(8,128)(2,1)}), bf16[16,17,8,128]{3,2,1,0:T(8,128)(2,1)S(1)}, u32[]{:S(2)}, u32[]{:S(2)}) async-start(bf16[16,17,8,128]{3,2,1,0:T(8,128)(2,1)} %add_factors.1), calls=%async_computation | async-start | bytes 1114112 | tf_op jit(solution)/shard_map/all_to_all | solution.py:350
  20.4 0.0 copy-done.3
  20.4 0.7 reshape.7.l_ref
  21.1 0.0 copy-start.2
  21.1 10.5 %all-to-all-done.r_ref = bf16[16,17,8,128]{3,2,1,0:T(8,128)(2,1)S(1)} async-done(((bf16[16,17,8,128]{3,2,1,0:T(8,128)(2,1)}), bf16[16,17,8,128]{3,2,1,0:T(8,128)(2,1)S(1)}, u32[]{:S(2)}, u32[]{:S(2)}) %all-to-all-start) | async-done | bytes 557088 | tf_op jit(solution)/shard_map/all_to_all | solution.py:350
  31.6 0.0 copy-start
  31.6 0.8 %copy-done = bf16[16,17,8,128]{3,2,1,0:T(8,128)(2,1)} copy-done((bf16[16,17,8,128]{3,2,1,0:T(8,128)(2,1)}, bf16[16,17,8,128]{3,2,1,0:T(8,128)(2,1)S(1)}, u32[]{:S(2)}) %copy-start) | copy-done | bytes 557080
  32.4 2.0 %image_part.1 = f32[16,8,256]{2,1,0:T(8,128)} custom-call(bf16[16,17,8,128]{3,2,1,0:T(8,128)(2,1)} %copy-done, bf16[256,256]{1,0:T(8,128)(2,1)} %reshape.7.l_ref), custom_call_target="tpu_custom_call" | custom-call | tf_op jit(solution)/shard_map/image_part/pallas_call | solution.py:166
  34.4 8.2 %all-to-all-start.1 = ((f32[16,8,256]{2,1,0:T(8,128)}), f32[16,8,256]{2,1,0:T(8,128)S(1)}, u32[]{:S(2)}, u32[]{:S(2)}) async-start(f32[16,8,256]{2,1,0:T(8,128)} %image_part.1), calls=%async_computation.1 | async-start | bytes 262144 | tf_op jit(solution)/shard_map/all_to_all | solution.py:350
  42.6 0.0 copy-done.2
  42.6 0.9 %reshape.6.s_ref = bf16[2,4,8,4096]{3,2,1,0:T(8,128)(2,1)} reshape(bf16[2,8,4,4096]{3,2,1,0:T(4,128)(2,1)S(1)} %copy-done.2) | data formatting | bytes 1048576 | tf_op jit(solution)/shard_map/reshape | solution.py:362
  43.5 2.8 %prepare_part.1 = (bf16[256,128]{1,0:T(8,128)(2,1)}, f32[16,16,8,128]{3,2,1,0:T(8,128)}) custom-call(bf16[16,17,8,128]{3,2,1,0:T(8,128)(2,1)} %copy-done), custom_call_target="tpu_custom_call" | custom-call | tf_op jit(solution)/shard_map/prepare_part/pallas_call | solution.py:197
  46.4 5.6 %all-to-all-done.1.i_ref = f32[16,8,256]{2,1,0:T(8,128)S(1)} async-done(((f32[16,8,256]{2,1,0:T(8,128)}), f32[16,8,256]{2,1,0:T(8,128)S(1)}, u32[]{:S(2)}, u32[]{:S(2)}) %all-to-all-start.1) | async-done | bytes 131104 | tf_op jit(solution)/shard_map/all_to_all | solution.py:350
  52.0 0.0 copy-start.1
  52.0 0.7 copy-done.1
  52.7 8.2 %main_part.1 = f32[16,8,256]{2,1,0:T(8,128)} custom-call(bf16[2,4,8,4096]{3,2,1,0:T(8,128)(2,1)} %reshape.6.s_ref, f32[16,8,256]{2,1,0:T(8,128)} %copy-done.1, f32[16,16,8,128]{3,2,1,0:T(8,128)} %get-tuple-element.8.z_ref, bf16[2,256,256]{2,1,0:T(8,128)(2,1)} %constant.7.clone.f_ref, bf16[2,256,256]{2,1,0:T(8,128)(2,1)} %constant.8.clone.b_ref), custom_call_target="tpu_custom_call" | custom-call | tf_op jit(solution)/shard_map/main_part/pallas_call | solution.py:308
  60.9 14.3 %all_to_all.15.c_ref = f32[16,8,256]{2,1,0:T(8,128)} all-to-all(f32[16,8,256]{2,1,0:T(8,128)} %main_part.1), channel_id=1, replica_groups=mesh['vox'=16,'tm'=16] {'tm'}, dimensions={0} | all-to-all | bytes 262144 | tf_op jit(solution)/shard_map/all_to_all | solution.py:350
  75.2 1.9 %last_part.1 = f32[32,2,4,256]{3,2,1,0:T(4,128)} custom-call(bf16[256,128]{1,0:T(8,128)(2,1)} %get-tuple-element.7.w_ref, f32[16,8,256]{2,1,0:T(8,128)} %all_to_all.15.c_ref), custom_call_target="tpu_custom_call" | custom-call | tf_op jit(solution)/shard_map/last_part/pallas_call | solution.py:340
Async XLA Ops:
  0.7 4.7 %collective-permute-start = (bf16[2,1,32]{2,1,0:T(2,128)(2,1)S(1)}, bf16[2,1,32]{2,1,0:T(2,128)(2,1)S(1)}, u32[]{:S(2)}, u32[]{:S(2)}) collective-permute-start(bf16[2,1,32]{2,1,0:T(2,128)(2,1)S(1)} %copy.10), channel_id=1, source_target_pairs={{0,0},{1,1},{2,2},{3,3},{4,4},{5,5},{6,6},{7,7},{8,8},{9,9},{10,10... | collective-permute-start | bytes 392 | tf_op jit(solution)/shard_map/ppermute | solution.py:355
  5.3 0.6 copy-start.4
  7.3 13.1 %copy-start.3 = (bf16[32,2,4,256]{3,2,1,0:T(4,128)(2,1)S(1)}, bf16[32,2,4,256]{3,2,1,0:T(4,128)(2,1)}, u32[]{:S(2)}) copy-start(bf16[32,2,4,256]{3,2,1,0:T(4,128)(2,1)} %param.8) | copy-start | bytes 393220
  7.3 24.3 %all-to-all-start = ((bf16[16,17,8,128]{3,2,1,0:T(8,128)(2,1)}), bf16[16,17,8,128]{3,2,1,0:T(8,128)(2,1)S(1)}, u32[]{:S(2)}, u32[]{:S(2)}) async-start(bf16[16,17,8,128]{3,2,1,0:T(8,128)(2,1)} %add_factors.1), calls=%async_computation | async-start | bytes 1114112 | tf_op jit(solution)/shard_map/all_to_all | solution.py:350
  21.1 21.5 %copy-start.2 = (bf16[2,8,4,4096]{3,2,1,0:T(4,128)(2,1)S(1)}, bf16[2,8,4,4096]{3,2,1,0:T(4,128)(2,1)}, u32[]{:S(2)}) copy-start(bf16[2,8,4,4096]{3,2,1,0:T(4,128)(2,1)} %param.10) | copy-start | bytes 1572868
  31.6 0.8 %copy-start = (bf16[16,17,8,128]{3,2,1,0:T(8,128)(2,1)}, bf16[16,17,8,128]{3,2,1,0:T(8,128)(2,1)S(1)}, u32[]{:S(2)}) copy-start(bf16[16,17,8,128]{3,2,1,0:T(8,128)(2,1)S(1)} %all-to-all-done.r_ref) | copy-start | bytes 1671172
  34.4 17.6 %all-to-all-start.1 = ((f32[16,8,256]{2,1,0:T(8,128)}), f32[16,8,256]{2,1,0:T(8,128)S(1)}, u32[]{:S(2)}, u32[]{:S(2)}) async-start(f32[16,8,256]{2,1,0:T(8,128)} %image_part.1), calls=%async_computation.1 | async-start | bytes 262144 | tf_op jit(solution)/shard_map/all_to_all | solution.py:350
  52.0 0.7 copy-start.1

commit v2 on v1

--- a/solution.py
+++ b/solution.py
@@ -103,7 +103,7 @@
             pl.BlockSpec((2, 256, 256), lambda q: (0, 0, 0)),
         ],
         out_specs=pl.BlockSpec((16, 4, 8, 128), lambda q: (0, q, 0, 0)),
-        out_shape=jax.ShapeDtypeStruct((16, 17, 8, 128), BF16),
+        out_shape=pltpu.VMEM((16, 17, 8, 128), BF16),
         name="z_part",
     )(kspace, mask, jnp.asarray(x_table()))
 
@@ -111,8 +111,8 @@
 def factor_kernel(r_ref, z_ref, o_ref, row_ref, tile_ref, sem):
     del z_ref
     row_ref[...] = jnp.zeros_like(row_ref)
-    row_ref[0:1, :32] = r_ref[0].astype(F32)
-    row_ref[1:2, :32] = r_ref[1].astype(F32)
+    row_ref[0:1, :32] = r_ref[0, 0:1].astype(F32)
+    row_ref[1:2, :32] = r_ref[0, 1:2].astype(F32)
     re = jnp.broadcast_to(row_ref[0:1, :], (8, 128))
     im = jnp.broadcast_to(row_ref[1:2, :], (8, 128))
     upper = iota((8, 128), 0) < 4
@@ -128,7 +128,7 @@
         factor_kernel,
         in_specs=[VMEM, pl.BlockSpec(memory_space=pl.ANY)],
         out_specs=pl.BlockSpec(memory_space=pl.ANY),
-        out_shape=jax.ShapeDtypeStruct((16, 17, 8, 128), BF16),
+        out_shape=pltpu.VMEM((16, 17, 8, 128), BF16),
         scratch_shapes=[
             pltpu.VMEM((8, 128), F32),
             pltpu.VMEM((16, 1, 8, 128), BF16),
@@ -136,7 +136,7 @@
         ],
         input_output_aliases={1: 0},
         name="add_factors",
-    )(factors, z)
+    )(near(factors), near(z))
 
 
 def iota(shape, dim):
@@ -167,9 +167,9 @@
         image_kernel,
         in_specs=[VMEM, VMEM],
         out_specs=VMEM,
-        out_shape=jax.ShapeDtypeStruct((16, 8, 256), F32),
+        out_shape=pltpu.VMEM((16, 8, 256), F32),
         name="image_part",
-    )(received, spatial)
+    )(near(received), near(spatial))
 
 
 def prepare_kernel(r_ref, w_ref, z_ref):
@@ -199,11 +199,11 @@
         in_specs=[VMEM],
         out_specs=[VMEM, VMEM],
         out_shape=[
-            jax.ShapeDtypeStruct((256, 128), BF16),
-            jax.ShapeDtypeStruct((16, 16, 8, 128), F32),
+            pltpu.VMEM((256, 128), BF16),
+            pltpu.VMEM((16, 16, 8, 128), F32),
         ],
         name="prepare_part",
-    )(received)
+    )(near(received))
 
 
 def dft8(x, turn):
@@ -316,14 +316,14 @@
             table,
         ],
         out_specs=VMEM,
-        out_shape=jax.ShapeDtypeStruct((16, 8, 256), F32),
+        out_shape=pltpu.VMEM((16, 8, 256), F32),
         scratch_shapes=[
             pltpu.VMEM((256, 256), F32),
             pltpu.VMEM((64, 8, 128), F32),
             pltpu.VMEM((16, 2, 8, 256), F32),
         ],
         name="main_part",
-    )(sens, images, z, jnp.asarray(fwd), jnp.asarray(inv))
+    )(sens, near(images), near(z), jnp.asarray(fwd), jnp.asarray(inv))
 
 
 def last_kernel(w_ref, c_ref, o_ref):
@@ -343,7 +343,11 @@
         out_specs=VMEM,
         out_shape=jax.ShapeDtypeStruct((32, 2, 4, 256), F32),
         name="last_part",
-    )(weights, combined)
+    )(near(weights), near(combined))
+
+
+def near(value):
+    return pltpu.with_memory_space_constraint(value, pltpu.VMEM)
 
 
 def exchange(value, axis):
@@ -352,7 +356,7 @@
 
 def per_device(spatial, temporal, coil_sens, kspace, sample_mask):
     skew = [(j * 16 + (t + j) % 16, j * 16 + t) for j in range(16) for t in range(16)]
-    factors = lax.ppermute(temporal, ("vox", "tm"), skew)
+    factors = lax.ppermute(temporal.transpose(1, 0, 2), ("vox", "tm"), skew)
     z = z_part(kspace, sample_mask)
     z = add_factors(factors, z)
     received = exchange(z, "vox")

time: 77.6 us -> 70.7 us (0.911)
  Pallas kernels: 20.3 us -> 14.6 us
  local copies, waits for them, and re-layouts: 4.34 us -> 1.63 us
  waiting for transfers between devices: 16.1 us -> 18.8 us
  blocking collectives: 14.3 us -> 13.2 us
    all_to_all x2, waiting for transfers between devices: 16.1 us -> 18.8 us  [exchange(): return lax.all_to_all(value, axis, split_axis=0, concat_axis=0, tiled=True)]
    unnamed x11 -> x6, local copies, waits for them, and re-layouts: 2.72 us -> 0.67 us
    pallas_call x1, Pallas kernels: 2.84 us -> 0.81 us  [prepare_part(): pl.pallas_call(prepare_kernel, in_specs=[VMEM], out_specs=[VMEM, VMEM], o...]
    all_to_all x1, blocking collectives: 14.3 us -> 13.2 us  [exchange(): return lax.all_to_all(value, axis, split_axis=0, concat_axis=0, tiled=True)]
    pallas_call x1, Pallas kernels: 2.01 us -> 0.95 us  [image_part(): pl.pallas_call(image_kernel, in_specs=[VMEM, VMEM], out_specs=VMEM, out_s...]
    pallas_call x1, Pallas kernels: 8.24 us -> 7.25 us  [main_part(): pl.pallas_call(main_kernel, grid=(4,), in_specs=[pl.BlockSpec((2, 1, 8, 4...]
    pallas_call x1, Pallas kernels: 1.86 us -> 0.92 us  [last_part(): pl.pallas_call(last_kernel, in_specs=[VMEM, VMEM], out_specs=VMEM, out_sh...]
  transfers between devices with their start and end apart: 3 -> 3, of which waited for: 2 -> 2; matrix products, arithmetic and copies ran while one was open for 2% -> 1% of each run, Pallas kernels for 9% -> 7%
where the time goes in v2:
time: 70.7 us; the launch traced here: 70.3 us
  starting transfers between devices  21.9 us (31%)
  waiting for transfers between devices  18.8 us (27%)
  Pallas kernels  14.6 us (21%)
  blocking collectives  13.2 us (19%)
  local copies, waits for them, and re-layouts  1.63 us (2%)
    all_to_all x2, starting transfers between devices, exchange(): return lax.all_to_all(value, axis, split_axis=0, concat_axis=0, tiled=True)  21.3 us
    all_to_all x2, waiting for transfers between devices, exchange(): return lax.all_to_all(value, axis, split_axis=0, concat_axis=0, tiled=True)  18.8 us
    all_to_all x1, blocking collectives, exchange(): return lax.all_to_all(value, axis, split_axis=0, concat_axis=0, tiled=True)  13.2 us
    pallas_call x1, Pallas kernels, main_part(): pl.pallas_call(main_kernel, grid=(4,), in_specs=[pl.BlockSpec((2, 1, 8, 4...  7.25 us
    pallas_call x1, Pallas kernels, z_part(): pl.pallas_call(z_kernel, grid=(4,), in_specs=[pl.BlockSpec((2, 1, 2, 64,...  3.97 us
  transfers between devices with their start and end apart: 3, of which 2 were waited for; matrix products, arithmetic and copies ran while one was open for 1% of the time, Pallas kernels for 7%

profile of v2, /device:TPU:32, one launch (start us, length us, event | category | flops | bytes accessed | tf_op | source)
XLA Modules:
  0.0 70.3 jit_solution(7773302588282026074)
XLA Ops:
  0.0 0.0 copy-start.2
  0.0 0.7 copy-done.2
  0.7 0.6 collective-permute-start
  1.3 4.0 %z_part.1.z_ref = bf16[16,17,8,128]{3,2,1,0:T(8,128)(2,1)} custom-call(bf16[2,1,8,64,256]{4,3,2,1,0:T(8,128)(2,1)} %k_ref.1, s32[1,256]{1,0:T(1,128)} %m_ref.1, bf16[2,256,256]{2,1,0:T(8,128)(2,1)} %constant.6.clone.t_ref), custom_call_target="tpu_custom_call" | custom-call | tf_op jit(solution)/shard_map/z_part/pallas_call | solution.py:97
  5.3 0.0 collective-permute-done.r_ref
  5.3 0.7 %add_factors.1 = bf16[16,17,8,128]{3,2,1,0:T(8,128)(2,1)} custom-call(bf16[1,2,32]{2,1,0:T(2,128)(2,1)S(1)} %collective-permute-done.r_ref, bf16[16,17,8,128]{3,2,1,0:T(8,128)(2,1)} %z_part.1.z_ref), custom_call_target="tpu_custom_call", output_to_operand_aliasing={{}: (1, {})} | custom-call | tf_op jit(solution)/shard_map/add_factors/pallas_call | solution.py:127
  6.0 0.0 copy-start.1
  6.0 13.1 %all-to-all-start = ((bf16[16,17,8,128]{3,2,1,0:T(8,128)(2,1)}), bf16[16,17,8,128]{3,2,1,0:T(8,128)(2,1)S(1)}, u32[]{:S(2)}, u32[]{:S(2)}) async-start(bf16[16,17,8,128]{3,2,1,0:T(8,128)(2,1)} %add_factors.1), calls=%async_computation | async-start | bytes 1114112 | tf_op jit(solution)/shard_map/all_to_all | solution.py:354
  19.1 0.0 copy-done.1
  19.2 0.0 copy-start
  19.2 11.1 %all-to-all-done.r_ref = bf16[16,17,8,128]{3,2,1,0:T(8,128)(2,1)S(1)} async-done(((bf16[16,17,8,128]{3,2,1,0:T(8,128)(2,1)}), bf16[16,17,8,128]{3,2,1,0:T(8,128)(2,1)S(1)}, u32[]{:S(2)}, u32[]{:S(2)}) %all-to-all-start) | async-done | bytes 557088 | tf_op jit(solution)/shard_map/all_to_all | solution.py:354
  30.3 1.0 %image_part.1 = f32[16,8,256]{2,1,0:T(8,128)} custom-call(bf16[16,17,8,128]{3,2,1,0:T(8,128)(2,1)S(1)} %all-to-all-done.r_ref, bf16[256,256]{1,0:T(8,128)(2,1)S(1)} %reshape.7.l_ref), custom_call_target="tpu_custom_call" | custom-call | tf_op jit(solution)/shard_map/image_part/pallas_call | solution.py:166
  31.2 8.2 %all-to-all-start.1 = ((f32[16,8,256]{2,1,0:T(8,128)}), f32[16,8,256]{2,1,0:T(8,128)S(1)}, u32[]{:S(2)}, u32[]{:S(2)}) async-start(f32[16,8,256]{2,1,0:T(8,128)} %image_part.1), calls=%async_computation.1 | async-start | bytes 262144 | tf_op jit(solution)/shard_map/all_to_all | solution.py:354
  39.4 0.0 copy-done
  39.4 0.9 %reshape.6.s_ref = bf16[2,4,8,4096]{3,2,1,0:T(8,128)(2,1)} reshape(bf16[2,8,4,4096]{3,2,1,0:T(4,128)(2,1)S(1)} %copy-done) | data formatting | bytes 1048576 | tf_op jit(solution)/shard_map/reshape | solution.py:366
  40.4 0.8 %prepare_part.1 = (bf16[256,128]{1,0:T(8,128)(2,1)S(1)}, f32[16,16,8,128]{3,2,1,0:T(8,128)S(1)}) custom-call(bf16[16,17,8,128]{3,2,1,0:T(8,128)(2,1)S(1)} %all-to-all-done.r_ref), custom_call_target="tpu_custom_call" | custom-call | tf_op jit(solution)/shard_map/prepare_part/pallas_call | solution.py:197
  41.2 7.7 %all-to-all-done.1.i_ref = f32[16,8,256]{2,1,0:T(8,128)S(1)} async-done(((f32[16,8,256]{2,1,0:T(8,128)}), f32[16,8,256]{2,1,0:T(8,128)S(1)}, u32[]{:S(2)}, u32[]{:S(2)}) %all-to-all-start.1) | async-done | bytes 131104 | tf_op jit(solution)/shard_map/all_to_all | solution.py:354
  48.8 7.2 %main_part.1 = f32[16,8,256]{2,1,0:T(8,128)S(1)} custom-call(bf16[2,4,8,4096]{3,2,1,0:T(8,128)(2,1)} %reshape.6.s_ref, f32[16,8,256]{2,1,0:T(8,128)S(1)} %all-to-all-done.1.i_ref, f32[16,16,8,128]{3,2,1,0:T(8,128)S(1)} %get-tuple-element.8.z_ref, bf16[2,256,256]{2,1,0:T(8,128)(2,1)} %constant.7.clone.f_ref, bf16[2,256,256]{2,1,0:T(8,128)(2,1)} %constant.8.clone.b_ref), custom_call_target="tpu_custom_call" | custom-call | tf_op jit(solution)/shard_map/main_part/pallas_call | solution.py:308
  56.1 13.2 %all_to_all.15.c_ref = f32[16,8,256]{2,1,0:T(8,128)S(1)} all-to-all(f32[16,8,256]{2,1,0:T(8,128)S(1)} %main_part.1), channel_id=1, replica_groups=mesh['vox'=16,'tm'=16] {'tm'}, dimensions={0} | all-to-all | bytes 262144 | tf_op jit(solution)/shard_map/all_to_all | solution.py:354
  69.3 0.9 %last_part.1 = f32[32,2,4,256]{3,2,1,0:T(4,128)} custom-call(bf16[256,128]{1,0:T(8,128)(2,1)S(1)} %get-tuple-element.7.w_ref, f32[16,8,256]{2,1,0:T(8,128)S(1)} %all_to_all.15.c_ref), custom_call_target="tpu_custom_call" | custom-call | tf_op jit(solution)/shard_map/last_part/pallas_call | solution.py:340
  (1 shorter events, 0.0 us)
Async XLA Ops:
  0.0 0.7 copy-start.2
  0.7 4.6 %collective-permute-start = (bf16[1,2,32]{2,1,0:T(2,128)(2,1)S(1)}, bf16[1,2,32]{2,1,0:T(2,128)(2,1)S(1)}, u32[]{:S(2)}, u32[]{:S(2)}) collective-permute-start(bf16[1,2,32]{2,1,0:T(2,128)(2,1)S(1)} %bitcast.1), channel_id=1, source_target_pairs={{0,0},{1,1},{2,2},{3,3},{4,4},{5,5},{6,6},{7,7},{8,8},{9,9},{10,10... | collective-permute-start | bytes 392 | tf_op jit(solution)/shard_map/ppermute | solution.py:359
  6.0 13.1 %copy-start.1 = (bf16[32,2,4,256]{3,2,1,0:T(4,128)(2,1)S(1)}, bf16[32,2,4,256]{3,2,1,0:T(4,128)(2,1)}, u32[]{:S(2)}) copy-start(bf16[32,2,4,256]{3,2,1,0:T(4,128)(2,1)} %param.8) | copy-start | bytes 393220
  6.0 24.3 %all-to-all-start = ((bf16[16,17,8,128]{3,2,1,0:T(8,128)(2,1)}), bf16[16,17,8,128]{3,2,1,0:T(8,128)(2,1)S(1)}, u32[]{:S(2)}, u32[]{:S(2)}) async-start(bf16[16,17,8,128]{3,2,1,0:T(8,128)(2,1)} %add_factors.1), calls=%async_computation | async-start | bytes 1114112 | tf_op jit(solution)/shard_map/all_to_all | solution.py:354
  19.2 20.3 %copy-start = (bf16[2,8,4,4096]{3,2,1,0:T(4,128)(2,1)S(1)}, bf16[2,8,4,4096]{3,2,1,0:T(4,128)(2,1)}, u32[]{:S(2)}) copy-start(bf16[2,8,4,4096]{3,2,1,0:T(4,128)(2,1)} %param.10) | copy-start | bytes 1572868
  31.2 17.6 %all-to-all-start.1 = ((f32[16,8,256]{2,1,0:T(8,128)}), f32[16,8,256]{2,1,0:T(8,128)S(1)}, u32[]{:S(2)}, u32[]{:S(2)}) async-start(f32[16,8,256]{2,1,0:T(8,128)} %image_part.1), calls=%async_computation.1 | async-start | bytes 262144 | tf_op jit(solution)/shard_map/all_to_all | solution.py:354

commit v3 on v2

v3 whole, which is shorter than its diff:
```python
import math

import jax
import jax.numpy as jnp
import numpy as np
from jax import lax
from jax.experimental import pallas as pl
from jax.experimental.pallas import tpu as pltpu
from jax.sharding import PartitionSpec as P


N = 64
F32 = jnp.float32
BF16 = jnp.bfloat16
VMEM = pl.BlockSpec(memory_space=pltpu.VMEM)
HBM = pl.BlockSpec(memory_space=pl.ANY)
SMALL = pltpu.CompilerParams(vmem_limit_bytes=16 * 2**20)
CODE_SHIFT = 60.0
CODE_SCALE = 2.0**60
UNSEEN = 3e38
SEEN_BELOW = 1e37


def split(table):
    table = np.asarray(table, np.float64)
    high = table.astype(jnp.bfloat16)
    low = (table - high.astype(np.float64)).astype(jnp.bfloat16)
    return high, low


def dft64():
    k = np.arange(N)
    angle = 2.0 * np.pi * (np.outer(k, k) % N) / N
    return np.cos(angle), np.sin(angle)


def x_table():
    cos, sin = dft64()
    table = np.zeros((2, 16, 2, 4, 2, 2, N))
    for c in range(2):
        table[0, :, c, :, c, 0] = cos.reshape(16, 4, N)
        table[0, :, c, :, c, 1] = -sin.reshape(16, 4, N)
        table[1, :, c, :, c, 0] = sin.reshape(16, 4, N)
        table[1, :, c, :, c, 1] = cos.reshape(16, 4, N)
    return np.concatenate(split(table.reshape(256, 256) / 8.0), axis=1)


def z_tables():
    cos, sin = dft64()
    tables = []
    for sign in (1.0, -1.0):
        table = np.zeros((2, 2, N, 2, 2, N))
        for b in range(2):
            table[0, b, :, 0, b] = cos
            table[1, b, :, 0, b] = sign * sin
            table[0, b, :, 1, b] = -sign * sin
            table[1, b, :, 1, b] = cos
        high, low = split(table.reshape(256, 256) / 64.0)
        tables.append(np.concatenate([high, low], axis=0))
    return tables


def y_table():
    n, j, b = np.meshgrid(np.arange(4), np.arange(8), np.arange(128) // N, indexing="ij")
    angle = 2.0 * np.pi * ((2 * n + b) * j % N) / N
    return np.stack([np.cos(angle), np.sin(angle)], axis=2).reshape(64, 128).astype(np.float32)


def dot(a, b):
    return jnp.dot(a, b, preferred_element_type=F32)


def halves(value):
    high = value.astype(BF16)
    return high, (value - high.astype(F32)).astype(BF16)


def z_kernel(k_hbm, m_ref, t_hbm, o_ref, k_ref, t_ref, sems):
    copies = [pltpu.make_async_copy(t_hbm, t_ref, sems.at[4])]
    for q in range(4):
        pair = pl.ds(2 * q, 2)
        copies.append(pltpu.make_async_copy(k_hbm.at[:, :, pair], k_ref.at[:, :, pair], sems.at[q]))
    for copy in copies:
        copy.start()
    for copy in copies:
        copy.wait()
    seen = jnp.broadcast_to(m_ref[...].astype(F32), (8, 256)) > 0.5
    for q in range(4):
        data = [k_ref[part, 0, 2 * q + c] for c in range(2) for part in range(2)]
        out = dot(t_ref[...], jnp.concatenate(data + data, axis=0))
        even = out * out
        fourth = even * even
        even = fourth * fourth * even * CODE_SCALE
        out = jnp.where(out < 0.0, -even, even)
        for part in range(2):
            for h in range(2):
                lanes = slice(h * 128, h * 128 + 128)
                value = out[part * 128 : part * 128 + 128, lanes].reshape(16, 8, 128)
                value = jnp.where(seen[None, :, lanes], value, UNSEEN)
                o_ref[:, 4 * q + 2 * part + h] = value.astype(BF16)


def z_part(kspace, mask):
    return pl.pallas_call(
        z_kernel,
        in_specs=[HBM, VMEM, HBM],
        out_specs=VMEM,
        out_shape=pltpu.VMEM((16, 17, 8, 128), BF16),
        scratch_shapes=[
            pltpu.VMEM(kspace.shape, BF16),
            pltpu.VMEM((256, 512), BF16),
            pltpu.SemaphoreType.DMA((5,)),
        ],
        name="z_part",
        compiler_params=SMALL,
    )(far(kspace), near(mask), far(jnp.asarray(x_table())))


def factor_kernel(r_ref, z_ref, o_ref, row_ref, tile_ref, sem):
    del z_ref
    row_ref[...] = jnp.zeros_like(row_ref)
    row_ref[0:1, :32] = r_ref[0, 0:1].astype(F32)
    row_ref[1:2, :32] = r_ref[0, 1:2].astype(F32)
    re = jnp.broadcast_to(row_ref[0:1, :], (8, 128))
    im = jnp.broadcast_to(row_ref[1:2, :], (8, 128))
    upper = iota((8, 128), 0) < 4
    tile = jnp.where(upper, re, im) + pltpu.roll(jnp.where(upper, -im, re), 32, 1)
    tile_ref[...] = jnp.broadcast_to(tile.astype(BF16)[None, None], (16, 1, 8, 128))
    copy = pltpu.make_async_copy(tile_ref, o_ref.at[:, 16:17], sem)
    copy.start()
    copy.wait()


def add_factors(factors, z):
    return pl.pallas_call(
        factor_kernel,
        in_specs=[VMEM, pl.BlockSpec(memory_space=pl.ANY)],
        out_specs=pl.BlockSpec(memory_space=pl.ANY),
        out_shape=pltpu.VMEM((16, 17, 8, 128), BF16),
        scratch_shapes=[
            pltpu.VMEM((8, 128), F32),
            pltpu.VMEM((16, 1, 8, 128), BF16),
            pltpu.SemaphoreType.DMA,
        ],
        input_output_aliases={1: 0},
        name="add_factors",
        compiler_params=SMALL,
    )(near(factors), near(z))


def iota(shape, dim):
    return lax.broadcasted_iota(jnp.int32, shape, dim)


def one_hot(test):
    return jnp.where(test, 1.0, 0.0).astype(BF16)


def factor_rows(r_ref):
    t = lax.axis_index("tm")
    tiles = [r_ref[lax.rem(f - t + 16, 16), 16].astype(F32) for f in range(16)]
    return jnp.concatenate(tiles, axis=0).astype(BF16)


def image_kernel(r_ref, l_ref, o_ref):
    column = iota((128, 256), 1)
    pick = iota((128, 256), 0) == column // 8 + column // 4 % 2 * 32
    weights = dot(factor_rows(r_ref), one_hot(pick))
    same_x = iota((128, 256), 0) % 4 == column % 4
    weights = jnp.where(same_x, weights, 0.0).astype(BF16)
    o_ref[...] = dot(weights, l_ref[...]).reshape(16, 8, 256)


def image_part(received, spatial):
    return pl.pallas_call(
        image_kernel,
        in_specs=[VMEM, VMEM],
        out_specs=VMEM,
        out_shape=pltpu.VMEM((16, 8, 256), F32),
        name="image_part",
        compiler_params=SMALL,
    )(near(received), near(spatial))


def prepare_kernel(r_ref, w_ref, z_ref):
    row = iota((256, 128), 0)
    pick = iota((256, 128), 1) == row // 8 + row // 4 % 2 * 32
    weights = lax.dot_general(
        one_hot(pick), factor_rows(r_ref), (((1,), (1,)), ((), ())), preferred_element_type=F32
    )
    same_x = row % 4 == iota((256, 128), 1) % 4
    w_ref[...] = jnp.where(same_x, weights, 0.0).astype(BF16)

    low_half = iota((8, 128), 1) < N

    def decode(v, tile):
        code = r_ref[v, tile].astype(F32)
        size = jnp.abs(code)
        root = jnp.exp2((jnp.log2(size) - CODE_SHIFT) * 0.1)
        root = jnp.where(size > 0.0, root, 0.0)
        root = jnp.where(code < 0.0, -root, root)
        return jnp.where(size < SEEN_BELOW, root, UNSEEN)

    def pair(v, carry):
        for q in range(4):
            for part in range(2):
                for h in range(2):
                    a, b = decode(v, 4 * q + 2 * part + h), decode(v + 8, 4 * q + 2 * part + h)
                    z_ref[q, part, 4 * v + 2 * h] = jnp.where(low_half, a, pltpu.roll(b, N, 1))
                    z_ref[q, part, 4 * v + 2 * h + 1] = jnp.where(low_half, pltpu.roll(a, N, 1), b)
        return carry

    lax.fori_loop(0, 8, pair, 0)


def prepare_part(received):
    return pl.pallas_call(
        prepare_kernel,
        in_specs=[VMEM],
        out_specs=[VMEM, VMEM],
        out_shape=[
            pltpu.VMEM((256, 128), BF16),
            pltpu.VMEM((4, 2, 32, 8, 128), F32),
        ],
        name="prepare_part",
        compiler_params=SMALL,
    )(near(received))


def plus(a, b):
    return a[0] + b[0], a[1] + b[1]


def minus(a, b):
    return a[0] - b[0], a[1] - b[1]


def plus_i(a, b, sign):
    if sign > 0:
        return a[0] - b[1], a[1] + b[0]
    return a[0] + b[1], a[1] - b[0]


def times(a, c, s, sign):
    if sign > 0:
        return a[0] * c - a[1] * s, a[1] * c + a[0] * s
    return a[0] * c + a[1] * s, a[1] * c - a[0] * s


def dft4(x, sign):
    a, b, c, d = plus(x[0], x[2]), minus(x[0], x[2]), plus(x[1], x[3]), minus(x[1], x[3])
    return [plus(a, c), plus_i(b, d, sign), minus(a, c), plus_i(b, d, -sign)]


def dft8(x, sign):
    half = math.sqrt(0.5)
    e, o = dft4(x[0::2], sign), dft4(x[1::2], sign)
    p = plus_i(o[1], o[1], sign)
    m = plus_i(o[3], o[3], -sign)
    p = p[0] * half, p[1] * half
    m = m[0] * half, m[1] * half
    return [
        plus(e[0], o[0]),
        plus(e[1], p),
        plus_i(e[2], o[2], sign),
        minus(e[3], m),
        minus(e[0], o[0]),
        minus(e[1], p),
        plus_i(e[2], o[2], -sign),
        plus(e[3], m),
    ]


def main_kernel(s_ref, i_ref, z_ref, f_ref, b_ref, y_ref, o_ref, t_ref, u_ref, acc_ref):
    upper = iota((8, 256), 0) < 4
    low_half = iota((8, 128), 1) < N
    flip = jnp.where(low_half, 1.0, -1.0)
    cos1 = jnp.where(low_half, 1.0, math.sqrt(0.5))
    cos3 = jnp.where(low_half, 1.0, -math.sqrt(0.5))
    sin1 = jnp.where(low_half, 0.0, math.sqrt(0.5))

    def sens(q, part, yh, h):
        at = yh * 256 + h * 128
        return s_ref[part, q, :, at : at + 128].astype(F32)

    def along_z(value, table):
        high, low = halves(value)
        table = jnp.concatenate([table[:256], table[:256], table[256:]], axis=0)
        return dot(jnp.concatenate([high, low, high], axis=1), table)

    def coil_images(q):
        parts = ([], [])
        for h in range(2):
            for yh in range(16):
                both = i_ref[yh, :, h * 128 : h * 128 + 128]
                other = pltpu.roll(both, 4, 0)
                a = jnp.where(upper[:, :128], both, other)
                b = jnp.where(upper[:, :128], other, both)
                s_re, s_im = sens(q, 0, yh, h), sens(q, 1, yh, h)
                parts[0].append(s_re * a - s_im * b)
                parts[1].append(s_re * b + s_im * a)
        value = jnp.concatenate([jnp.concatenate(part, axis=0) for part in parts], axis=1)
        t_ref[q] = along_z(value, f_ref)

    def rows(m, n):
        at = n % 2 * 128 + (2 * m + n // 2) * 8
        return slice(at, at + 8)

    def turn(value, i, sign):
        if i == 0:
            return value
        if i == 2:
            re, im = value
            if sign > 0:
                return jnp.where(low_half, re, -im), jnp.where(low_half, im, re)
            return jnp.where(low_half, re, im), jnp.where(low_half, im, -re)
        return times(value, cos1 if i == 1 else cos3, sin1, sign)

    def wave(n, j):
        at = 2 * (8 * n + j)
        return y_ref[at : at + 1, :], y_ref[at + 1 : at + 2, :]

    def across(value):
        return tuple(part * flip + pltpu.roll(part, N, 1) for part in value)

    def residual(q):
        for n in range(4):
            x = [(t_ref[q, rows(m, n), :128], t_ref[q, rows(m, n), 128:]) for m in range(8)]
            x = dft8(x, -1)
            for j in range(8):
                if j > 0:
                    x[j] = times(x[j], *wave(n, j), -1)
                u_ref[q, 4 * j + n, 0], u_ref[q, 4 * j + n, 1] = x[j]
        for j in range(8):
            x = dft4([(u_ref[q, 4 * j + n, 0], u_ref[q, 4 * j + n, 1]) for n in range(4)], -1)
            for i in range(4):
                re, im = across(turn(x[i], i, -1))
                z_re, z_im = z_ref[q, 0, 8 * i + j], z_ref[q, 1, 8 * i + j]
                seen = z_re < SEEN_BELOW
                left = jnp.where(seen, re - z_re, 0.0), jnp.where(seen, im - z_im, 0.0)
                x[i] = turn(across(left), i, 1)
            x = dft4(x, 1)
            for n in range(4):
                if j > 0:
                    x[n] = times(x[n], *wave(n, j), 1)
                u_ref[q, 4 * j + n, 0], u_ref[q, 4 * j + n, 1] = x[n]
        for n in range(4):
            x = [(u_ref[q, 4 * j + n, 0], u_ref[q, 4 * j + n, 1]) for j in range(8)]
            x = dft8(x, 1)
            for m in range(8):
                t_ref[q, rows(m, n), :128], t_ref[q, rows(m, n), 128:] = x[m]

    def combine(q):
        value = along_z(t_ref[q], b_ref)
        for h in range(2):
            for yh in range(16):
                at = h * 128 + yh * 8
                a, b = value[at : at + 8, :128], value[at : at + 8, 128:]
                s_re, s_im = sens(q, 0, yh, h), sens(q, 1, yh, h)
                re = s_re * a + s_im * b
                im = s_re * b - s_im * a
                if q > 0:
                    re = re + acc_ref[yh, h, 0]
                    im = im + acc_ref[yh, h, 1]
                if q < 3:
                    acc_ref[yh, h, 0] = re
                    acc_ref[yh, h, 1] = im
                else:
                    re = re + pltpu.roll(re, 4, 0)
                    im = im + pltpu.roll(im, 4, 0)
                    o_ref[yh, :, h * 128 : h * 128 + 128] = jnp.where(upper[:, :128], re, im)

    coil_images(0)
    for q in range(4):
        if q < 3:
            coil_images(q + 1)
        residual(q)
        if q > 0:
            combine(q - 1)
    combine(3)


def main_part(sens, images, z):
    fwd, inv = z_tables()
    return pl.pallas_call(
        main_kernel,
        in_specs=[VMEM] * 6,
        out_specs=VMEM,
        out_shape=pltpu.VMEM((16, 8, 256), F32),
        scratch_shapes=[
            pltpu.VMEM((4, 256, 256), F32),
            pltpu.VMEM((4, 32, 2, 8, 128), F32),
            pltpu.VMEM((16, 2, 2, 8, 128), F32),
        ],
        name="main_part",
        compiler_params=SMALL,
    )(
        near(sens),
        near(images),
        near(z),
        near(jnp.asarray(fwd)),
        near(jnp.asarray(inv)),
        near(jnp.asarray(y_table())),
    )


def last_kernel(w_ref, c_ref, o_ref):
    high, low = halves(c_ref[...].reshape(128, 256))
    w = w_ref[...]
    out = dot(w, high) + dot(w, low)
    for r in range(32):
        for part in range(2):
            row = r * 8 + part * 4
            o_ref[r, part] = out[row : row + 4]


def last_part(weights, combined):
    return pl.pallas_call(
        last_kernel,
        in_specs=[VMEM, VMEM],
        out_specs=VMEM,
        out_shape=jax.ShapeDtypeStruct((32, 2, 4, 256), F32),
        name="last_part",
        compiler_params=SMALL,
    )(near(weights), near(combined))


def near(value):
    return pltpu.with_memory_space_constraint(value, pltpu.VMEM)


def far(value):
    return pltpu.with_memory_space_constraint(value, pltpu.HBM)


def exchange(value, axis):
    return lax.all_to_all(value, axis, split_axis=0, concat_axis=0, tiled=True)


def per_device(spatial, temporal, coil_sens, kspace, sample_mask):
    skew = [(j * 16 + (t + j) % 16, j * 16 + t) for j in range(16) for t in range(16)]
    factors = lax.ppermute(temporal.transpose(1, 0, 2), ("vox", "tm"), skew)
    z = z_part(kspace, sample_mask)
    z = add_factors(factors, z)
    received = exchange(z, "vox")
    images = image_part(received, spatial.reshape(256, 256))
    images = exchange(images, "tm")
    weights, z = prepare_part(received)
    combined = main_part(coil_sens.reshape(2, 4, 8, 4096), images, z)
    combined = exchange(combined, "tm")
    return last_part(weights, combined)


def solution(mesh):
    placed = (
        P(None, None, "vox", "tm"),
        P(None, "tm", None),
        P(None, None, "vox", None),
        P(None, "tm", None, None, "vox"),
        P("tm", "vox"),
    )
    return jax.shard_map(
        per_device,
        mesh=mesh,
        in_specs=placed,
        out_specs=P(None, None, "vox", "tm"),
        check_vma=False,
    )
```

time: 70.7 us -> 65.4 us (0.925)
  Pallas kernels: 14.6 us -> 8.41 us
  starting transfers between devices: 21.9 us -> 23.3 us
  local copies, waits for them, and re-layouts: 1.63 us -> 0.85 us
    pallas_call x2, Pallas kernels: 11.2 us -> 4.55 us  [the longest x1 2.58 us: z_part(): pl.pallas_call(z_kernel, in_specs=[HBM, VMEM, HBM], out_specs=VMEM, out_s...]
    all_to_all x2, starting transfers between devices: 21.3 us -> 22.6 us  [exchange(): return lax.all_to_all(value, axis, split_axis=0, concat_axis=0, tiled=True)]
    reshape x1, local copies, waits for them, and re-layouts: 0.92 us -> 0.12 us  [per_device(): combined = main_part(coil_sens.reshape(2, 4, 8, 4096), images, z)]
  transfers between devices with their start and end apart: 3 -> 3, of which waited for: 2 -> 2; matrix products, arithmetic and copies ran while one was open for 1% -> 0% of each run, Pallas kernels for 7% -> 6%
where the time goes in v3:
time: 65.4 us; the launch traced here: 65 us
  starting transfers between devices  23.3 us (36%)
  waiting for transfers between devices  19.1 us (29%)
  blocking collectives  13.2 us (20%)
  Pallas kernels  8.41 us (13%)
  local copies, waits for them, and re-layouts  0.85 us (1%)
    all_to_all x2, starting transfers between devices, exchange(): return lax.all_to_all(value, axis, split_axis=0, concat_axis=0, tiled=True)  22.6 us
    all_to_all x2, waiting for transfers between devices, exchange(): return lax.all_to_all(value, axis, split_axis=0, concat_axis=0, tiled=True)  19.1 us
    all_to_all x1, blocking collectives, exchange(): return lax.all_to_all(value, axis, split_axis=0, concat_axis=0, tiled=True)  13.2 us
    pallas_call x1, Pallas kernels, z_part(): pl.pallas_call(z_kernel, in_specs=[HBM, VMEM, HBM], out_specs=VMEM, out_s...  2.58 us
    pallas_call x1, Pallas kernels, main_part(): pl.pallas_call(main_kernel, in_specs=[VMEM] * 6, out_specs=VMEM, out_shap...  1.97 us
  transfers between devices with their start and end apart: 3, of which 2 were waited for; matrix products, arithmetic and copies ran while one was open for 0% of the time, Pallas kernels for 6%

profile of v3, /device:TPU:32, one launch (start us, length us, event | category | flops | bytes accessed | tf_op | source)
XLA Modules:
  0.0 65.0 jit_solution(18107742316507615970)
XLA Ops:
  0.0 0.0 copy-start.6
  0.0 0.0 copy-start.3
  0.0 0.7 %copy-done.6 = bf16[2,1,32]{2,0,1:T(2,128)(2,1)S(1)} copy-done((bf16[2,1,32]{2,0,1:T(2,128)(2,1)S(1)}, bf16[2,1,32]{2,0,1:T(2,128)(2,1)}, u32[]{:S(2)}) %copy-start.6) | copy-done | bytes 152
  0.7 0.6 collective-permute-start
  1.3 0.0 copy-done.3
  1.3 2.6 %z_part.1.z_ref = bf16[16,17,8,128]{3,2,1,0:T(8,128)(2,1)} custom-call(bf16[2,1,8,64,256]{4,3,2,1,0:T(8,128)(2,1)} %k_hbm.1, s32[1,256]{1,0:T(1,128)S(1)} %copy-done.3, bf16[256,512]{1,0:T(8,128)(2,1)} %constant.8.clone.t_hbm), custom_call_target="tpu_custom_call" | custom-call | tf_op jit(solution)/shard_map/z_part/pallas_call | solution.py:104
  3.9 0.0 collective-permute-done.r_ref
  3.9 0.7 %add_factors.1 = bf16[16,17,8,128]{3,2,1,0:T(8,128)(2,1)} custom-call(bf16[1,2,32]{2,1,0:T(2,128)(2,1)S(1)} %collective-permute-done.r_ref, bf16[16,17,8,128]{3,2,1,0:T(8,128)(2,1)} %z_part.1.z_ref), custom_call_target="tpu_custom_call", output_to_operand_aliasing={{}: (1, {})} | custom-call | tf_op jit(solution)/shard_map/add_factors/pallas_call | solution.py:135
  4.7 0.0 copy-start.5
  4.7 13.5 %all-to-all-start = ((bf16[16,17,8,128]{3,2,1,0:T(8,128)(2,1)}), bf16[16,17,8,128]{3,2,1,0:T(8,128)(2,1)S(1)}, u32[]{:S(2)}, u32[]{:S(2)}) async-start(bf16[16,17,8,128]{3,2,1,0:T(8,128)(2,1)} %add_factors.1), calls=%async_computation | async-start | bytes 1114112 | tf_op jit(solution)/shard_map/all_to_all | solution.py:437
  18.1 0.0 copy-done.5
  18.2 0.0 copy-start.4
  18.2 11.1 %all-to-all-done.r_ref = bf16[16,17,8,128]{3,2,1,0:T(8,128)(2,1)S(1)} async-done(((bf16[16,17,8,128]{3,2,1,0:T(8,128)(2,1)}), bf16[16,17,8,128]{3,2,1,0:T(8,128)(2,1)S(1)}, u32[]{:S(2)}, u32[]{:S(2)}) %all-to-all-start) | async-done | bytes 557088 | tf_op jit(solution)/shard_map/all_to_all | solution.py:437
  29.3 1.0 %image_part.1 = f32[16,8,256]{2,1,0:T(8,128)} custom-call(bf16[16,17,8,128]{3,2,1,0:T(8,128)(2,1)S(1)} %all-to-all-done.r_ref, bf16[256,256]{1,0:T(8,128)(2,1)S(1)} %reshape.7.l_ref), custom_call_target="tpu_custom_call" | custom-call | tf_op jit(solution)/shard_map/image_part/pallas_call | solution.py:175
  30.3 9.2 %all-to-all-start.1 = ((f32[16,8,256]{2,1,0:T(8,128)}), f32[16,8,256]{2,1,0:T(8,128)S(1)}, u32[]{:S(2)}, u32[]{:S(2)}) async-start(f32[16,8,256]{2,1,0:T(8,128)} %image_part.1), calls=%async_computation.1 | async-start | bytes 262144 | tf_op jit(solution)/shard_map/all_to_all | solution.py:437
  39.4 0.0 copy-done.4
  39.5 0.1 reshape.6.s_ref
  39.6 0.0 copy-start
  39.6 0.0 copy-start.1
  39.6 0.0 copy-start.2
  39.6 1.3 %prepare_part.1 = (bf16[256,128]{1,0:T(8,128)(2,1)S(1)}, f32[4,2,32,8,128]{4,3,2,1,0:T(8,128)S(1)}) custom-call(bf16[16,17,8,128]{3,2,1,0:T(8,128)(2,1)S(1)} %all-to-all-done.r_ref), custom_call_target="tpu_custom_call" | custom-call | tf_op jit(solution)/shard_map/prepare_part/pallas_call | solution.py:217
  40.9 8.0 %all-to-all-done.1.i_ref = f32[16,8,256]{2,1,0:T(8,128)S(1)} async-done(((f32[16,8,256]{2,1,0:T(8,128)}), f32[16,8,256]{2,1,0:T(8,128)S(1)}, u32[]{:S(2)}, u32[]{:S(2)}) %all-to-all-start.1) | async-done | bytes 131104 | tf_op jit(solution)/shard_map/all_to_all | solution.py:437
  48.9 0.0 copy-done
  48.9 0.0 copy-done.1
  48.9 0.0 copy-done.2
  48.9 2.0 %main_part.1 = f32[16,8,256]{2,1,0:T(8,128)S(1)} custom-call(bf16[2,4,8,4096]{3,2,1,0:T(8,128)(2,1)S(1)} %reshape.6.s_ref, f32[16,8,256]{2,1,0:T(8,128)S(1)} %all-to-all-done.1.i_ref, f32[4,2,32,8,128]{4,3,2,1,0:T(8,128)S(1)} %get-tuple-element.8.z_ref, bf16[512,256]{1,0:T(8,128)(2,1)S(1)} %copy-done.1, bf16[512,256]{1,0:T(8,128)(2,1)S(1)} %copy-done, ...), custom_call_target="tpu_custom_call" | custom-call | tf_op jit(solution)/shard_map/main_part/pallas_call | solution.py:385
  50.8 13.2 %all_to_all.15.c_ref = f32[16,8,256]{2,1,0:T(8,128)S(1)} all-to-all(f32[16,8,256]{2,1,0:T(8,128)S(1)} %main_part.1), channel_id=1, replica_groups=mesh['vox'=16,'tm'=16] {'tm'}, dimensions={0} | all-to-all | bytes 262144 | tf_op jit(solution)/shard_map/all_to_all | solution.py:437
  64.1 0.9 %last_part.1 = f32[32,2,4,256]{3,2,1,0:T(4,128)} custom-call(bf16[256,128]{1,0:T(8,128)(2,1)S(1)} %get-tuple-element.7.w_ref, f32[16,8,256]{2,1,0:T(8,128)S(1)} %all_to_all.15.c_ref), custom_call_target="tpu_custom_call" | custom-call | tf_op jit(solution)/shard_map/last_part/pallas_call | solution.py:418
  (1 shorter events, 0.0 us)
Async XLA Ops:
  0.0 0.7 %copy-start.6 = (bf16[2,1,32]{2,0,1:T(2,128)(2,1)S(1)}, bf16[2,1,32]{2,0,1:T(2,128)(2,1)}, u32[]{:S(2)}) copy-start(bf16[2,1,32]{2,0,1:T(2,128)(2,1)} %param.10) | copy-start | bytes 388
  0.0 1.3 %copy-start.3 = (s32[1,256]{1,0:T(1,128)S(1)}, s32[1,256]{1,0:T(1,128)}, u32[]{:S(2)}) copy-start(s32[1,256]{1,0:T(1,128)} %m_ref.1) | copy-start | bytes 3076
  0.7 3.3 %collective-permute-start = (bf16[1,2,32]{2,1,0:T(2,128)(2,1)S(1)}, bf16[1,2,32]{2,1,0:T(2,128)(2,1)S(1)}, u32[]{:S(2)}, u32[]{:S(2)}) collective-permute-start(bf16[1,2,32]{2,1,0:T(2,128)(2,1)S(1)} %bitcast.1), channel_id=1, source_target_pairs={{0,0},{1,1},{2,2},{3,3},{4,4},{5,5},{6,6},{7,7},{8,8},{9,9},{10,10... | collective-permute-start | bytes 392 | tf_op jit(solution)/shard_map/ppermute | solution.py:442
  4.7 13.5 %copy-start.5 = (bf16[32,2,4,256]{3,2,1,0:T(4,128)(2,1)S(1)}, bf16[32,2,4,256]{3,2,1,0:T(4,128)(2,1)}, u32[]{:S(2)}) copy-start(bf16[32,2,4,256]{3,2,1,0:T(4,128)(2,1)} %param.9) | copy-start | bytes 393220
  4.7 24.6 %all-to-all-start = ((bf16[16,17,8,128]{3,2,1,0:T(8,128)(2,1)}), bf16[16,17,8,128]{3,2,1,0:T(8,128)(2,1)S(1)}, u32[]{:S(2)}, u32[]{:S(2)}) async-start(bf16[16,17,8,128]{3,2,1,0:T(8,128)(2,1)} %add_factors.1), calls=%async_computation | async-start | bytes 1114112 | tf_op jit(solution)/shard_map/all_to_all | solution.py:437
  18.2 21.3 %copy-start.4 = (bf16[2,8,4,4096]{3,2,1,0:T(4,128)(2,1)S(1)}, bf16[2,8,4,4096]{3,2,1,0:T(4,128)(2,1)}, u32[]{:S(2)}) copy-start(bf16[2,8,4,4096]{3,2,1,0:T(4,128)(2,1)} %param.11) | copy-start | bytes 1572868
  30.3 18.6 %all-to-all-start.1 = ((f32[16,8,256]{2,1,0:T(8,128)}), f32[16,8,256]{2,1,0:T(8,128)S(1)}, u32[]{:S(2)}, u32[]{:S(2)}) async-start(f32[16,8,256]{2,1,0:T(8,128)} %image_part.1), calls=%async_computation.1 | async-start | bytes 262144 | tf_op jit(solution)/shard_map/all_to_all | solution.py:437
  39.6 9.3 %copy-start = (bf16[512,256]{1,0:T(8,128)(2,1)S(1)}, bf16[512,256]{1,0:T(8,128)(2,1)}, u32[]{:S(2)}) copy-start(bf16[512,256]{1,0:T(8,128)(2,1)} %constant.10.clone.b_ref) | copy-start | bytes 786436
  39.6 9.3 %copy-start.1 = (bf16[512,256]{1,0:T(8,128)(2,1)S(1)}, bf16[512,256]{1,0:T(8,128)(2,1)}, u32[]{:S(2)}) copy-start(bf16[512,256]{1,0:T(8,128)(2,1)} %constant.9.clone.f_ref) | copy-start | bytes 786436
  39.6 9.3 %copy-start.2 = (f32[64,128]{1,0:T(8,128)S(1)}, f32[64,128]{1,0:T(8,128)}, u32[]{:S(2)}) copy-start(f32[64,128]{1,0:T(8,128)} %constant.11.clone.y_ref) | copy-start | bytes 98308

commit v4 on v3

--- a/solution.py
+++ b/solution.py
@@ -15,8 +15,7 @@
 VMEM = pl.BlockSpec(memory_space=pltpu.VMEM)
 HBM = pl.BlockSpec(memory_space=pl.ANY)
 SMALL = pltpu.CompilerParams(vmem_limit_bytes=16 * 2**20)
-CODE_SHIFT = 60.0
-CODE_SCALE = 2.0**60
+Z_SCALE = 2.0**6
 UNSEEN = 3e38
 SEEN_BELOW = 1e37
 
@@ -42,7 +41,7 @@
         table[0, :, c, :, c, 1] = -sin.reshape(16, 4, N)
         table[1, :, c, :, c, 0] = sin.reshape(16, 4, N)
         table[1, :, c, :, c, 1] = cos.reshape(16, 4, N)
-    return np.concatenate(split(table.reshape(256, 256) / 8.0), axis=1)
+    return np.concatenate(split(table.reshape(256, 256) / 8.0 * Z_SCALE), axis=1)
 
 
 def z_tables():
@@ -75,23 +74,63 @@
     return high, (value - high.astype(F32)).astype(BF16)
 
 
-def z_kernel(k_hbm, m_ref, t_hbm, o_ref, k_ref, t_ref, sems):
-    copies = [pltpu.make_async_copy(t_hbm, t_ref, sems.at[4])]
-    for q in range(4):
-        pair = pl.ds(2 * q, 2)
-        copies.append(pltpu.make_async_copy(k_hbm.at[:, :, pair], k_ref.at[:, :, pair], sems.at[q]))
+def load_kernel(l_hbm, k_hbm, m_hbm, t_hbm, l_ref, k_ref, m_ref, t_ref, s_ref, sems):
+    copies = [
+        pltpu.make_async_copy(l_hbm, s_ref, sems.at[0]),
+        pltpu.make_async_copy(m_hbm, m_ref, sems.at[1]),
+        pltpu.make_async_copy(t_hbm, t_ref, sems.at[2]),
+        pltpu.make_async_copy(k_hbm, k_ref, sems.at[3]),
+    ]
     for copy in copies:
         copy.start()
-    for copy in copies:
+    copies[0].wait()
+    for r in range(0, 32, 2):
+        rows = [s_ref[r + i // 2, i % 2].astype(F32) for i in range(4)]
+        l_ref[8 * r : 8 * r + 16] = jnp.concatenate(rows, axis=0).astype(BF16)
+    for copy in copies[1:]:
         copy.wait()
+
+
+def load_part(spatial, kspace, mask):
+    return pl.pallas_call(
+        load_kernel,
+        in_specs=[HBM] * 4,
+        out_specs=[VMEM] * 4,
+        out_shape=[
+            pltpu.VMEM((256, 256), BF16),
+            pltpu.VMEM(kspace.shape, BF16),
+            pltpu.VMEM((1, 256), jnp.int32),
+            pltpu.VMEM((256, 512), BF16),
+        ],
+        scratch_shapes=[
+            pltpu.VMEM(spatial.shape, BF16),
+            pltpu.SemaphoreType.DMA((4,)),
+        ],
+        name="load_part",
+        compiler_params=SMALL,
+    )(far(spatial), far(kspace), far(mask), far(jnp.asarray(x_table())))
+
+
+def encode(value):
+    even = value * value
+    fourth = even * even
+    even = fourth * fourth * even
+    return jnp.where(value < 0.0, -even, even)
+
+
+def decode(code, scale):
+    size = jnp.abs(code)
+    root = jnp.exp2(jnp.log2(size) * 0.1 - math.log2(scale))
+    root = jnp.where(size > 0.0, root, 0.0)
+    return jnp.where(code < 0.0, -root, root)
+
+
+def z_kernel(k_ref, m_ref, t_ref, o_ref):
     seen = jnp.broadcast_to(m_ref[...].astype(F32), (8, 256)) > 0.5
     for q in range(4):
         data = [k_ref[part, 0, 2 * q + c] for c in range(2) for part in range(2)]
         out = dot(t_ref[...], jnp.concatenate(data + data, axis=0))
-        even = out * out
-        fourth = even * even
-        even = fourth * fourth * even * CODE_SCALE
-        out = jnp.where(out < 0.0, -even, even)
+        out = encode(out)
         for part in range(2):
             for h in range(2):
                 lanes = slice(h * 128, h * 128 + 128)
@@ -100,52 +139,15 @@
                 o_ref[:, 4 * q + 2 * part + h] = value.astype(BF16)
 
 
-def z_part(kspace, mask):
+def z_part(kspace, mask, table):
     return pl.pallas_call(
         z_kernel,
-        in_specs=[HBM, VMEM, HBM],
+        in_specs=[VMEM, VMEM, VMEM],
         out_specs=VMEM,
         out_shape=pltpu.VMEM((16, 17, 8, 128), BF16),
-        scratch_shapes=[
-            pltpu.VMEM(kspace.shape, BF16),
-            pltpu.VMEM((256, 512), BF16),
-            pltpu.SemaphoreType.DMA((5,)),
-        ],
         name="z_part",
         compiler_params=SMALL,
-    )(far(kspace), near(mask), far(jnp.asarray(x_table())))
-
-
-def factor_kernel(r_ref, z_ref, o_ref, row_ref, tile_ref, sem):
-    del z_ref
-    row_ref[...] = jnp.zeros_like(row_ref)
-    row_ref[0:1, :32] = r_ref[0, 0:1].astype(F32)
-    row_ref[1:2, :32] = r_ref[0, 1:2].astype(F32)
-    re = jnp.broadcast_to(row_ref[0:1, :], (8, 128))
-    im = jnp.broadcast_to(row_ref[1:2, :], (8, 128))
-    upper = iota((8, 128), 0) < 4
-    tile = jnp.where(upper, re, im) + pltpu.roll(jnp.where(upper, -im, re), 32, 1)
-    tile_ref[...] = jnp.broadcast_to(tile.astype(BF16)[None, None], (16, 1, 8, 128))
-    copy = pltpu.make_async_copy(tile_ref, o_ref.at[:, 16:17], sem)
-    copy.start()
-    copy.wait()
-
-
-def add_factors(factors, z):
-    return pl.pallas_call(
-        factor_kernel,
-        in_specs=[VMEM, pl.BlockSpec(memory_space=pl.ANY)],
-        out_specs=pl.BlockSpec(memory_space=pl.ANY),
-        out_shape=pltpu.VMEM((16, 17, 8, 128), BF16),
-        scratch_shapes=[
-            pltpu.VMEM((8, 128), F32),
-            pltpu.VMEM((16, 1, 8, 128), BF16),
-            pltpu.SemaphoreType.DMA,
-        ],
-        input_output_aliases={1: 0},
-        name="add_factors",
-        compiler_params=SMALL,
-    )(near(factors), near(z))
+    )(near(kspace), near(mask), near(table))
 
 
 def iota(shape, dim):
@@ -158,7 +160,16 @@
 
 def factor_rows(r_ref):
     t = lax.axis_index("tm")
-    tiles = [r_ref[lax.rem(f - t + 16, 16), 16].astype(F32) for f in range(16)]
+    upper = iota((8, 128), 0) < 4
+    first = iota((8, 128), 1) < 32
+    tiles = []
+    for f in range(16):
+        ahead = lax.rem(f - t + 16, 8)
+        flip = lax.rem(f // 8 + t // 8, 2)
+        raw = r_ref[ahead * 2 + flip, 16].astype(F32)
+        re = jnp.broadcast_to(raw[0:1], (8, 128))
+        im = jnp.broadcast_to(raw[1:2], (8, 128))
+        tiles.append(jnp.where(first, jnp.where(upper, re, im), pltpu.roll(jnp.where(upper, -im, re), 32, 1)))
     return jnp.concatenate(tiles, axis=0).astype(BF16)
 
 
@@ -193,19 +204,15 @@
 
     low_half = iota((8, 128), 1) < N
 
-    def decode(v, tile):
+    def value(v, tile):
         code = r_ref[v, tile].astype(F32)
-        size = jnp.abs(code)
-        root = jnp.exp2((jnp.log2(size) - CODE_SHIFT) * 0.1)
-        root = jnp.where(size > 0.0, root, 0.0)
-        root = jnp.where(code < 0.0, -root, root)
-        return jnp.where(size < SEEN_BELOW, root, UNSEEN)
+        return jnp.where(jnp.abs(code) < SEEN_BELOW, decode(code, Z_SCALE), UNSEEN)
 
     def pair(v, carry):
         for q in range(4):
             for part in range(2):
                 for h in range(2):
-                    a, b = decode(v, 4 * q + 2 * part + h), decode(v + 8, 4 * q + 2 * part + h)
+                    a, b = value(v, 4 * q + 2 * part + h), value(v + 8, 4 * q + 2 * part + h)
                     z_ref[q, part, 4 * v + 2 * h] = jnp.where(low_half, a, pltpu.roll(b, N, 1))
                     z_ref[q, part, 4 * v + 2 * h + 1] = jnp.where(low_half, pltpu.roll(a, N, 1), b)
         return carry
@@ -437,13 +444,23 @@
     return lax.all_to_all(value, axis, split_axis=0, concat_axis=0, tiled=True)
 
 
+def sources():
+    pairs = []
+    for j in range(16):
+        for t in range(16):
+            half, place = t // 8 ^ j % 2, (t + j // 2) % 8
+            source = j ^ 2 if j % 2 else j
+            pairs.append((source * 16 + half * 8 + place, j * 16 + t))
+    return pairs
+
+
 def per_device(spatial, temporal, coil_sens, kspace, sample_mask):
-    skew = [(j * 16 + (t + j) % 16, j * 16 + t) for j in range(16) for t in range(16)]
-    factors = lax.ppermute(temporal.transpose(1, 0, 2), ("vox", "tm"), skew)
-    z = z_part(kspace, sample_mask)
-    z = add_factors(factors, z)
+    factors = lax.ppermute(temporal.transpose(1, 0, 2), ("vox", "tm"), sources())
+    spatial, kspace, mask, table = load_part(spatial, kspace, sample_mask)
+    z = z_part(kspace, mask, table)
+    z = z.at[:, 16].set(jnp.pad(factors[0], ((0, 6), (0, 96))))
     received = exchange(z, "vox")
-    images = image_part(received, spatial.reshape(256, 256))
+    images = image_part(received, spatial)
     images = exchange(images, "tm")
     weights, z = prepare_part(received)
     combined = main_part(coil_sens.reshape(2, 4, 8, 4096), images, z)

time: 65.4 us -> 64 us (0.979)
  blocking collectives: 13.2 us -> 37.3 us
  starting transfers between devices: 23.3 us -> 10.1 us
  waiting for transfers between devices: 19.1 us -> 8.25 us
  Pallas kernels: 8.41 us -> 7.05 us
    all_to_all x1 -> x2, blocking collectives: 13.2 us -> 37.3 us  [exchange(): return lax.all_to_all(value, axis, split_axis=0, concat_axis=0, tiled=True)]
    all_to_all x2 -> x1, starting transfers between devices: 22.6 us -> 9.5 us  [exchange(): return lax.all_to_all(value, axis, split_axis=0, concat_axis=0, tiled=True)]
    all_to_all x2 -> x1, waiting for transfers between devices: 19.1 us -> 8.25 us  [exchange(): return lax.all_to_all(value, axis, split_axis=0, concat_axis=0, tiled=True)]
    pallas_call x2, Pallas kernels: 3.31 us -> 1.8 us  [the longest x1 1.25 us: load_part(): pl.pallas_call(load_kernel, in_specs=[HBM] * 4, out_specs=[VMEM] * 4, out...]
  transfers between devices with their start and end apart: 3 -> 2, of which waited for: 2 -> 1; matrix products, arithmetic and copies ran while one was open for 0% -> 0% of each run, Pallas kernels for 6% -> 5%
where the time goes in v4:
time: 64 us; the launch traced here: 63.7 us
  blocking collectives  37.3 us (58%)
  starting transfers between devices  10.1 us (16%)
  waiting for transfers between devices  8.25 us (13%)
  Pallas kernels  7.05 us (11%)
  local copies, waits for them, and re-layouts  0.82 us (1%)
    all_to_all x2, blocking collectives, exchange(): return lax.all_to_all(value, axis, split_axis=0, concat_axis=0, tiled=True)  37.3 us
    all_to_all x1, starting transfers between devices, exchange(): return lax.all_to_all(value, axis, split_axis=0, concat_axis=0, tiled=True)  9.5 us
    all_to_all x1, waiting for transfers between devices, exchange(): return lax.all_to_all(value, axis, split_axis=0, concat_axis=0, tiled=True)  8.25 us
    pallas_call x1, Pallas kernels, main_part(): pl.pallas_call(main_kernel, in_specs=[VMEM] * 6, out_specs=VMEM, out_shap...  1.97 us
    pallas_call x1, Pallas kernels, prepare_part(): pl.pallas_call(prepare_kernel, in_specs=[VMEM], out_specs=[VMEM, VMEM], o...  1.35 us
  transfers between devices with their start and end apart: 2, of which 1 were waited for; matrix products, arithmetic and copies ran while one was open for 0% of the time, Pallas kernels for 5%

profile of v4, /device:TPU:32, one launch (start us, length us, event | category | flops | bytes accessed | tf_op | source)
XLA Modules:
  0.0 63.7 jit_solution(7314071668913381083)
XLA Ops:
  0.0 0.0 copy-start.4
  0.0 0.7 %copy-done.4 = bf16[2,1,32]{2,0,1:T(2,128)(2,1)S(1)} copy-done((bf16[2,1,32]{2,0,1:T(2,128)(2,1)S(1)}, bf16[2,1,32]{2,0,1:T(2,128)(2,1)}, u32[]{:S(2)}) %copy-start.4) | copy-done | bytes 152
  0.7 0.6 %collective-permute-start = (bf16[1,2,32]{2,1,0:T(2,128)(2,1)S(1)}, bf16[1,2,32]{2,1,0:T(2,128)(2,1)S(1)}, u32[]{:S(2)}, u32[]{:S(2)}) collective-permute-start(bf16[1,2,32]{2,1,0:T(2,128)(2,1)S(1)} %bitcast.3), channel_id=1, source_target_pairs={{0,0},{1,1},{2,2},{3,3},{4,4},{5,5},{6,6},{7,7},{8,8},{9,9},{10,10... | collective-permute-start | bytes 392 | tf_op jit(solution)/shard_map/ppermute | solution.py:458
  1.3 1.2 %load_part.1 = (bf16[256,256]{1,0:T(8,128)(2,1)S(1)}, bf16[2,1,8,64,256]{4,3,2,1,0:T(8,128)(2,1)S(1)}, s32[1,256]{1,0:T(1,128)S(1)}, bf16[256,512]{1,0:T(8,128)(2,1)S(1)}) custom-call(bf16[32,2,4,256]{3,2,1,0:T(4,128)(2,1)} %l_hbm.1, bf16[2,1,8,64,256]{4,3,2,1,0:T(8,128)(2,1)} %k_hbm.1, s32[1,256]{1,0:T(1,128)} %m_hbm.1, bf16[256,512]{1,0:T(8,128)(2,1)} %constant.40.clone.t_hbm), custom_call_target="tpu_custom_call" | custom-call | tf_op jit(solution)/shard_map/load_part/pallas_call | solution.py:95
  2.6 0.5 z_part.1
  3.1 0.0 collective-permute-done
  3.2 24.2 %all_to_all.15.r_ref = bf16[16,17,8,128]{3,2,1,0:T(8,128)(2,1)S(1)} all-to-all(bf16[16,17,8,128]{3,2,1,0:T(8,128)(2,1)S(1)} %broadcast_dynamic-update-slice_fusion), channel_id=1, replica_groups=mesh['vox'=16,'tm'=16] {'vox'}, dimensions={0} | all-to-all | bytes 1114112 | tf_op jit(solution)/shard_map/all_to_all | solution.py:444
  27.4 0.0 copy-start.3
  27.4 1.0 %image_part.1 = f32[16,8,256]{2,1,0:T(8,128)} custom-call(bf16[16,17,8,128]{3,2,1,0:T(8,128)(2,1)S(1)} %all_to_all.15.r_ref, bf16[256,256]{1,0:T(8,128)(2,1)S(1)} %get-tuple-element.27.l_ref), custom_call_target="tpu_custom_call" | custom-call | tf_op jit(solution)/shard_map/image_part/pallas_call | solution.py:186
  28.4 9.5 %all-to-all-start.1 = ((f32[16,8,256]{2,1,0:T(8,128)}), f32[16,8,256]{2,1,0:T(8,128)S(1)}, u32[]{:S(2)}, u32[]{:S(2)}) async-start(f32[16,8,256]{2,1,0:T(8,128)} %image_part.1), calls=%async_computation.1 | async-start | bytes 262144 | tf_op jit(solution)/shard_map/all_to_all | solution.py:444
  37.9 0.0 copy-done.3
  37.9 0.1 reshape.35.s_ref
  38.1 0.0 copy-start
  38.1 0.0 copy-start.1
  38.1 0.0 copy-start.2
  38.1 1.3 %prepare_part.1 = (bf16[256,128]{1,0:T(8,128)(2,1)S(1)}, f32[4,2,32,8,128]{4,3,2,1,0:T(8,128)S(1)}) custom-call(bf16[16,17,8,128]{3,2,1,0:T(8,128)(2,1)S(1)} %all_to_all.15.r_ref), custom_call_target="tpu_custom_call" | custom-call | tf_op jit(solution)/shard_map/prepare_part/pallas_call | solution.py:224
  39.5 8.2 %all-to-all-done.1.i_ref = f32[16,8,256]{2,1,0:T(8,128)S(1)} async-done(((f32[16,8,256]{2,1,0:T(8,128)}), f32[16,8,256]{2,1,0:T(8,128)S(1)}, u32[]{:S(2)}, u32[]{:S(2)}) %all-to-all-start.1) | async-done | bytes 131104 | tf_op jit(solution)/shard_map/all_to_all | solution.py:444
  47.7 0.0 copy-done
  47.7 0.0 copy-done.1
  47.7 0.0 copy-done.2
  47.7 2.0 %main_part.1 = f32[16,8,256]{2,1,0:T(8,128)S(1)} custom-call(bf16[2,4,8,4096]{3,2,1,0:T(8,128)(2,1)S(1)} %reshape.35.s_ref, f32[16,8,256]{2,1,0:T(8,128)S(1)} %all-to-all-done.1.i_ref, f32[4,2,32,8,128]{4,3,2,1,0:T(8,128)S(1)} %get-tuple-element.28.z_ref, bf16[512,256]{1,0:T(8,128)(2,1)S(1)} %copy-done, bf16[512,256]{1,0:T(8,128)(2,1)S(1)} %copy-done.1, ...), custom_call_target="tpu_custom_call" | custom-call | tf_op jit(solution)/shard_map/main_part/pallas_call | solution.py:392
  49.7 13.1 %all_to_all.16.c_ref = f32[16,8,256]{2,1,0:T(8,128)S(1)} all-to-all(f32[16,8,256]{2,1,0:T(8,128)S(1)} %main_part.1), channel_id=1, replica_groups=mesh['vox'=16,'tm'=16] {'tm'}, dimensions={0} | all-to-all | bytes 262144 | tf_op jit(solution)/shard_map/all_to_all | solution.py:444
  62.8 0.9 %last_part.1 = f32[32,2,4,256]{3,2,1,0:T(4,128)} custom-call(bf16[256,128]{1,0:T(8,128)(2,1)S(1)} %get-tuple-element.26.w_ref, f32[16,8,256]{2,1,0:T(8,128)S(1)} %all_to_all.16.c_ref), custom_call_target="tpu_custom_call" | custom-call | tf_op jit(solution)/shard_map/last_part/pallas_call | solution.py:425
  (2 shorter events, 0.0 us)
Async XLA Ops:
  0.0 0.7 %copy-start.4 = (bf16[2,1,32]{2,0,1:T(2,128)(2,1)S(1)}, bf16[2,1,32]{2,0,1:T(2,128)(2,1)}, u32[]{:S(2)}) copy-start(bf16[2,1,32]{2,0,1:T(2,128)(2,1)} %param.12) | copy-start | bytes 388
  0.7 2.5 %collective-permute-start = (bf16[1,2,32]{2,1,0:T(2,128)(2,1)S(1)}, bf16[1,2,32]{2,1,0:T(2,128)(2,1)S(1)}, u32[]{:S(2)}, u32[]{:S(2)}) collective-permute-start(bf16[1,2,32]{2,1,0:T(2,128)(2,1)S(1)} %bitcast.3), channel_id=1, source_target_pairs={{0,0},{1,1},{2,2},{3,3},{4,4},{5,5},{6,6},{7,7},{8,8},{9,9},{10,10... | collective-permute-start | bytes 392 | tf_op jit(solution)/shard_map/ppermute | solution.py:458
  27.4 10.5 %copy-start.3 = (bf16[2,8,4,4096]{3,2,1,0:T(4,128)(2,1)S(1)}, bf16[2,8,4,4096]{3,2,1,0:T(4,128)(2,1)}, u32[]{:S(2)}) copy-start(bf16[2,8,4,4096]{3,2,1,0:T(4,128)(2,1)} %param.13) | copy-start | bytes 1572868
  28.4 19.3 %all-to-all-start.1 = ((f32[16,8,256]{2,1,0:T(8,128)}), f32[16,8,256]{2,1,0:T(8,128)S(1)}, u32[]{:S(2)}, u32[]{:S(2)}) async-start(f32[16,8,256]{2,1,0:T(8,128)} %image_part.1), calls=%async_computation.1 | async-start | bytes 262144 | tf_op jit(solution)/shard_map/all_to_all | solution.py:444
  38.1 9.6 %copy-start = (bf16[512,256]{1,0:T(8,128)(2,1)S(1)}, bf16[512,256]{1,0:T(8,128)(2,1)}, u32[]{:S(2)}) copy-start(bf16[512,256]{1,0:T(8,128)(2,1)} %constant.41.clone.f_ref) | copy-start | bytes 786436
  38.1 9.6 %copy-start.1 = (bf16[512,256]{1,0:T(8,128)(2,1)S(1)}, bf16[512,256]{1,0:T(8,128)(2,1)}, u32[]{:S(2)}) copy-start(bf16[512,256]{1,0:T(8,128)(2,1)} %constant.42.clone.b_ref) | copy-start | bytes 786436
  38.1 9.6 %copy-start.2 = (f32[64,128]{1,0:T(8,128)S(1)}, f32[64,128]{1,0:T(8,128)}, u32[]{:S(2)}) copy-start(f32[64,128]{1,0:T(8,128)} %constant.43.clone.y_ref) | copy-start | bytes 98308

commit v5 on v4

--- a/solution.py
+++ b/solution.py
@@ -16,6 +16,7 @@
 HBM = pl.BlockSpec(memory_space=pl.ANY)
 SMALL = pltpu.CompilerParams(vmem_limit_bytes=16 * 2**20)
 Z_SCALE = 2.0**6
+IMAGE_SCALE = 2.0**4
 UNSEEN = 3e38
 SEEN_BELOW = 1e37
 
@@ -179,7 +180,7 @@
     weights = dot(factor_rows(r_ref), one_hot(pick))
     same_x = iota((128, 256), 0) % 4 == column % 4
     weights = jnp.where(same_x, weights, 0.0).astype(BF16)
-    o_ref[...] = dot(weights, l_ref[...]).reshape(16, 8, 256)
+    o_ref[...] = encode(dot(weights, l_ref[...]) * IMAGE_SCALE).reshape(16, 8, 256).astype(BF16)
 
 
 def image_part(received, spatial):
@@ -187,7 +188,7 @@
         image_kernel,
         in_specs=[VMEM, VMEM],
         out_specs=VMEM,
-        out_shape=pltpu.VMEM((16, 8, 256), F32),
+        out_shape=pltpu.VMEM((16, 8, 256), BF16),
         name="image_part",
         compiler_params=SMALL,
     )(near(received), near(spatial))
@@ -278,7 +279,7 @@
     ]
 
 
-def main_kernel(s_ref, i_ref, z_ref, f_ref, b_ref, y_ref, o_ref, t_ref, u_ref, acc_ref):
+def main_kernel(s_ref, i_ref, z_ref, f_ref, b_ref, y_ref, o_ref, x_ref, t_ref, u_ref, acc_ref):
     upper = iota((8, 256), 0) < 4
     low_half = iota((8, 128), 1) < N
     flip = jnp.where(low_half, 1.0, -1.0)
@@ -299,7 +300,7 @@
         parts = ([], [])
         for h in range(2):
             for yh in range(16):
-                both = i_ref[yh, :, h * 128 : h * 128 + 128]
+                both = x_ref[yh, :, h * 128 : h * 128 + 128]
                 other = pltpu.roll(both, 4, 0)
                 a = jnp.where(upper[:, :128], both, other)
                 b = jnp.where(upper[:, :128], other, both)
@@ -377,6 +378,8 @@
                     im = im + pltpu.roll(im, 4, 0)
                     o_ref[yh, :, h * 128 : h * 128 + 128] = jnp.where(upper[:, :128], re, im)
 
+    for yh in range(16):
+        x_ref[yh] = decode(i_ref[yh].astype(F32), IMAGE_SCALE)
     coil_images(0)
     for q in range(4):
         if q < 3:
@@ -395,6 +398,7 @@
         out_specs=VMEM,
         out_shape=pltpu.VMEM((16, 8, 256), F32),
         scratch_shapes=[
+            pltpu.VMEM((16, 8, 256), F32),
             pltpu.VMEM((4, 256, 256), F32),
             pltpu.VMEM((4, 32, 2, 8, 128), F32),
             pltpu.VMEM((16, 2, 2, 8, 128), F32),

time: 64 us -> 63.2 us (0.988)
  waiting for transfers between devices: 8.25 us -> 7.54 us
    all_to_all x1, waiting for transfers between devices: 8.25 us -> 7.54 us  [exchange(): return lax.all_to_all(value, axis, split_axis=0, concat_axis=0, tiled=True)]
where the time goes in v5:
time: 63.2 us; the launch traced here: 63 us
  blocking collectives  37.3 us (59%)
  starting transfers between devices  10.1 us (16%)
  waiting for transfers between devices  7.54 us (12%)
  Pallas kernels  7.09 us (11%)
  local copies, waits for them, and re-layouts  0.82 us (1%)
    all_to_all x2, blocking collectives, exchange(): return lax.all_to_all(value, axis, split_axis=0, concat_axis=0, tiled=True)  37.3 us
    all_to_all x1, starting transfers between devices, exchange(): return lax.all_to_all(value, axis, split_axis=0, concat_axis=0, tiled=True)  9.5 us
    all_to_all x1, waiting for transfers between devices, exchange(): return lax.all_to_all(value, axis, split_axis=0, concat_axis=0, tiled=True)  7.54 us
    pallas_call x1, Pallas kernels, main_part(): pl.pallas_call(main_kernel, in_specs=[VMEM] * 6, out_specs=VMEM, out_shap...  2.02 us
    pallas_call x1, Pallas kernels, prepare_part(): pl.pallas_call(prepare_kernel, in_specs=[VMEM], out_specs=[VMEM, VMEM], o...  1.35 us
  transfers between devices with their start and end apart: 2, of which 1 were waited for; matrix products, arithmetic and copies ran while one was open for 0% of the time, Pallas kernels for 5%

profile of v5, /device:TPU:32, one launch (start us, length us, event | category | flops | bytes accessed | tf_op | source)
XLA Modules:
  0.0 63.0 jit_solution(4495621468181131641)
XLA Ops:
  0.0 0.0 copy-start.4
  0.0 0.7 %copy-done.4 = bf16[2,1,32]{2,0,1:T(2,128)(2,1)S(1)} copy-done((bf16[2,1,32]{2,0,1:T(2,128)(2,1)S(1)}, bf16[2,1,32]{2,0,1:T(2,128)(2,1)}, u32[]{:S(2)}) %copy-start.4) | copy-done | bytes 152
  0.7 0.6 %collective-permute-start = (bf16[1,2,32]{2,1,0:T(2,128)(2,1)S(1)}, bf16[1,2,32]{2,1,0:T(2,128)(2,1)S(1)}, u32[]{:S(2)}, u32[]{:S(2)}) collective-permute-start(bf16[1,2,32]{2,1,0:T(2,128)(2,1)S(1)} %bitcast.3), channel_id=1, source_target_pairs={{0,0},{1,1},{2,2},{3,3},{4,4},{5,5},{6,6},{7,7},{8,8},{9,9},{10,10... | collective-permute-start | bytes 392 | tf_op jit(solution)/shard_map/ppermute | solution.py:462
  1.3 1.2 %load_part.1 = (bf16[256,256]{1,0:T(8,128)(2,1)S(1)}, bf16[2,1,8,64,256]{4,3,2,1,0:T(8,128)(2,1)S(1)}, s32[1,256]{1,0:T(1,128)S(1)}, bf16[256,512]{1,0:T(8,128)(2,1)S(1)}) custom-call(bf16[32,2,4,256]{3,2,1,0:T(4,128)(2,1)} %l_hbm.1, bf16[2,1,8,64,256]{4,3,2,1,0:T(8,128)(2,1)} %k_hbm.1, s32[1,256]{1,0:T(1,128)} %m_hbm.1, bf16[256,512]{1,0:T(8,128)(2,1)} %constant.40.clone.t_hbm), custom_call_target="tpu_custom_call" | custom-call | tf_op jit(solution)/shard_map/load_part/pallas_call | solution.py:96
  2.6 0.5 z_part.1
  3.1 0.0 collective-permute-done
  3.2 24.2 %all_to_all.15.r_ref = bf16[16,17,8,128]{3,2,1,0:T(8,128)(2,1)S(1)} all-to-all(bf16[16,17,8,128]{3,2,1,0:T(8,128)(2,1)S(1)} %broadcast_dynamic-update-slice_fusion), channel_id=1, replica_groups=mesh['vox'=16,'tm'=16] {'vox'}, dimensions={0} | all-to-all | bytes 1114112 | tf_op jit(solution)/shard_map/all_to_all | solution.py:448
  27.4 0.0 copy-start.3
  27.4 1.0 %image_part.1 = bf16[16,8,256]{2,1,0:T(8,128)(2,1)} custom-call(bf16[16,17,8,128]{3,2,1,0:T(8,128)(2,1)S(1)} %all_to_all.15.r_ref, bf16[256,256]{1,0:T(8,128)(2,1)S(1)} %get-tuple-element.27.l_ref), custom_call_target="tpu_custom_call" | custom-call | tf_op jit(solution)/shard_map/image_part/pallas_call | solution.py:187
  28.4 9.5 %all-to-all-start.1 = ((bf16[16,8,256]{2,1,0:T(8,128)(2,1)}), bf16[16,8,256]{2,1,0:T(8,128)(2,1)S(1)}, u32[]{:S(2)}, u32[]{:S(2)}) async-start(bf16[16,8,256]{2,1,0:T(8,128)(2,1)} %image_part.1), calls=%async_computation.1 | async-start | bytes 131072 | tf_op jit(solution)/shard_map/all_to_all | solution.py:448
  37.9 0.0 copy-done.3
  37.9 0.1 reshape.35.s_ref
  38.0 0.0 copy-start
  38.1 0.0 copy-start.1
  38.1 0.0 copy-start.2
  38.1 1.4 %prepare_part.1 = (bf16[256,128]{1,0:T(8,128)(2,1)S(1)}, f32[4,2,32,8,128]{4,3,2,1,0:T(8,128)S(1)}) custom-call(bf16[16,17,8,128]{3,2,1,0:T(8,128)(2,1)S(1)} %all_to_all.15.r_ref), custom_call_target="tpu_custom_call" | custom-call | tf_op jit(solution)/shard_map/prepare_part/pallas_call | solution.py:225
  39.4 7.5 %all-to-all-done.1.i_ref = bf16[16,8,256]{2,1,0:T(8,128)(2,1)S(1)} async-done(((bf16[16,8,256]{2,1,0:T(8,128)(2,1)}), bf16[16,8,256]{2,1,0:T(8,128)(2,1)S(1)}, u32[]{:S(2)}, u32[]{:S(2)}) %all-to-all-start.1) | async-done | bytes 65568 | tf_op jit(solution)/shard_map/all_to_all | solution.py:448
  47.0 0.0 copy-done
  47.0 0.0 copy-done.1
  47.0 0.0 copy-done.2
  47.0 2.0 %main_part.1 = f32[16,8,256]{2,1,0:T(8,128)S(1)} custom-call(bf16[2,4,8,4096]{3,2,1,0:T(8,128)(2,1)S(1)} %reshape.35.s_ref, bf16[16,8,256]{2,1,0:T(8,128)(2,1)S(1)} %all-to-all-done.1.i_ref, f32[4,2,32,8,128]{4,3,2,1,0:T(8,128)S(1)} %get-tuple-element.28.z_ref, bf16[512,256]{1,0:T(8,128)(2,1)S(1)} %copy-done, bf16[512,256]{1,0:T(8,128)(2,1)S(1)} %copy-done.1, ...), custom_call_target="tpu_custom_call" | custom-call | tf_op jit(solution)/shard_map/main_part/pallas_call | solution.py:395
  49.0 13.0 %all_to_all.16.c_ref = f32[16,8,256]{2,1,0:T(8,128)S(1)} all-to-all(f32[16,8,256]{2,1,0:T(8,128)S(1)} %main_part.1), channel_id=1, replica_groups=mesh['vox'=16,'tm'=16] {'tm'}, dimensions={0} | all-to-all | bytes 262144 | tf_op jit(solution)/shard_map/all_to_all | solution.py:448
  62.0 0.9 %last_part.1 = f32[32,2,4,256]{3,2,1,0:T(4,128)} custom-call(bf16[256,128]{1,0:T(8,128)(2,1)S(1)} %get-tuple-element.26.w_ref, f32[16,8,256]{2,1,0:T(8,128)S(1)} %all_to_all.16.c_ref), custom_call_target="tpu_custom_call" | custom-call | tf_op jit(solution)/shard_map/last_part/pallas_call | solution.py:429
  (2 shorter events, 0.0 us)
Async XLA Ops:
  0.0 0.7 %copy-start.4 = (bf16[2,1,32]{2,0,1:T(2,128)(2,1)S(1)}, bf16[2,1,32]{2,0,1:T(2,128)(2,1)}, u32[]{:S(2)}) copy-start(bf16[2,1,32]{2,0,1:T(2,128)(2,1)} %param.12) | copy-start | bytes 388
  0.7 2.5 %collective-permute-start = (bf16[1,2,32]{2,1,0:T(2,128)(2,1)S(1)}, bf16[1,2,32]{2,1,0:T(2,128)(2,1)S(1)}, u32[]{:S(2)}, u32[]{:S(2)}) collective-permute-start(bf16[1,2,32]{2,1,0:T(2,128)(2,1)S(1)} %bitcast.3), channel_id=1, source_target_pairs={{0,0},{1,1},{2,2},{3,3},{4,4},{5,5},{6,6},{7,7},{8,8},{9,9},{10,10... | collective-permute-start | bytes 392 | tf_op jit(solution)/shard_map/ppermute | solution.py:462
  27.4 10.5 %copy-start.3 = (bf16[2,8,4,4096]{3,2,1,0:T(4,128)(2,1)S(1)}, bf16[2,8,4,4096]{3,2,1,0:T(4,128)(2,1)}, u32[]{:S(2)}) copy-start(bf16[2,8,4,4096]{3,2,1,0:T(4,128)(2,1)} %param.13) | copy-start | bytes 1572868
  28.4 18.6 %all-to-all-start.1 = ((bf16[16,8,256]{2,1,0:T(8,128)(2,1)}), bf16[16,8,256]{2,1,0:T(8,128)(2,1)S(1)}, u32[]{:S(2)}, u32[]{:S(2)}) async-start(bf16[16,8,256]{2,1,0:T(8,128)(2,1)} %image_part.1), calls=%async_computation.1 | async-start | bytes 131072 | tf_op jit(solution)/shard_map/all_to_all | solution.py:448
  38.0 8.9 %copy-start = (bf16[512,256]{1,0:T(8,128)(2,1)S(1)}, bf16[512,256]{1,0:T(8,128)(2,1)}, u32[]{:S(2)}) copy-start(bf16[512,256]{1,0:T(8,128)(2,1)} %constant.41.clone.f_ref) | copy-start | bytes 786436
  38.1 8.9 %copy-start.1 = (bf16[512,256]{1,0:T(8,128)(2,1)S(1)}, bf16[512,256]{1,0:T(8,128)(2,1)}, u32[]{:S(2)}) copy-start(bf16[512,256]{1,0:T(8,128)(2,1)} %constant.42.clone.b_ref) | copy-start | bytes 786436
  38.1 8.9 %copy-start.2 = (f32[64,128]{1,0:T(8,128)S(1)}, f32[64,128]{1,0:T(8,128)}, u32[]{:S(2)}) copy-start(f32[64,128]{1,0:T(8,128)} %constant.43.clone.y_ref) | copy-start | bytes 98308
